TPU v7x, 32 devices: a whole 2x2x4 slice. The times are simulated.
32 devices in a mesh: shift: 2 (over y), row: 8 (over z, x), col: 2 (over core).
Axes of the slice: x: 2, y: 2, z: 4, core: 2. Of those that a mesh axis runs over, the one named last changes fastest.
Arguments:
- krylov_basis: float32 [128, 3, 8, 8, 128], P('shift', None, 'row', 'col'), parts along dimension 0, may hold values from -4000 to 4000, as said below
- regions: int32 [8, 8, 128], P('row', 'col'), may hold values from 0 to 7
- mu_table: float32 [8], replicated, may hold values from 0.5 to 2
- eps_table: float32 [8], replicated, may hold values from 1 to 4
- shift_value: float32 [2], P('shift'), parts along dimension 0, may hold values from 0.5 to 2
Outputs:
- orthonormal: float32 [128, 3, 8, 8, 128], P('shift', None, 'row', 'col'), parts along dimension 0
- upper_factor: float32 [128, 64], P('shift'), parts along dimension 0
- applied: float32 [128, 3, 8, 8, 128], P('shift', None, 'row', 'col'), parts along dimension 0
- projected: float32 [128, 64], P('shift'), parts along dimension 0
There are 2 independent parts, one for each index of `shift`. A program takes and returns all parts, laid end to end along the dimension named above; an argument that names none is the same for every part. Nothing has to cross between parts.
Inputs may be any that keep to these rules, and one draw needn't show every extreme that they name: `krylov_basis`: Real-valued entries.
All inputs are finite; a program needn't handle non-finite values.
Results may differ from a plain program's by a relative error of at most 0.000071.
Values sent between devices are 32-bit elements; how exact they have to be, the bound alone decides.
A program may use at most 64 MiB of HBM per device.

v0:
```python
import jax
import jax.numpy as jnp
from jax import lax
from jax.sharding import PartitionSpec as P


def shifted(x, axis, by):
    peers = lax.axis_size(axis)
    pairs = [(i, i + by) for i in range(peers) if 0 <= i + by < peers]
    return lax.ppermute(x, axis, pairs)


def padded(x, sides, width):
    for axis, dim in sides:
        peers, length = (lax.axis_size(axis), x.shape[dim])
        up = [(i, (i + 1) % peers) for i in range(peers - 1)]
        down = [(j, i) for i, j in up]
        last = lax.slice_in_dim(x, length - width, length, axis=dim)
        leading = lax.slice_in_dim(x, 0, width, axis=dim)
        before = lax.ppermute(last, axis, up)
        after = lax.ppermute(leading, axis, down)
        x = jnp.concatenate([before, x, after], axis=dim)
    return x


def forward_z(values):
    return jnp.pad(values[..., 1:], ((0, 0), (0, 0), (0, 0), (0, 1))) - values


def backward_z(values):
    return values - jnp.pad(values[..., :-1], ((0, 0), (0, 0), (0, 0), (1, 0)))


def operator_block(padded_field, coupling, permittivity, shift_scalar):
    cells_x = padded_field.shape[2] - 2
    cells_y = padded_field.shape[3] - 2
    field_x = padded_field[:, 0]
    field_y = padded_field[:, 1]
    field_z = padded_field[:, 2]

    def corner_part(values):
        return values[:, : cells_x + 1, : cells_y + 1]

    def forward_x(values):
        return values[:, 1 : cells_x + 2, : cells_y + 1] - corner_part(values)

    def forward_y(values):
        return values[:, : cells_x + 1, 1 : cells_y + 2] - corner_part(values)

    def forward_dz(values):
        return forward_z(corner_part(values))

    curl_x = forward_y(field_z) - forward_dz(field_y)
    curl_y = forward_dz(field_x) - forward_x(field_z)
    curl_z = forward_x(field_y) - forward_y(field_x)
    weighted_x = coupling * curl_x
    weighted_y = coupling * curl_y
    weighted_z = coupling * curl_z

    def backward_x(values):
        return values[:, 1:, 1:] - values[:, :-1, 1:]

    def backward_y(values):
        return values[:, 1:, 1:] - values[:, 1:, :-1]

    def backward_dz(values):
        return backward_z(values[:, 1:, 1:])

    result_x = backward_y(weighted_z) - backward_dz(weighted_y)
    result_y = backward_dz(weighted_x) - backward_x(weighted_z)
    result_z = backward_x(weighted_y) - backward_y(weighted_x)
    interior = padded_field[:, :, 1 : cells_x + 1, 1 : cells_y + 1]
    stacked = jnp.stack([result_x, result_y, result_z], axis=1)
    return stacked - shift_scalar * permittivity * interior


def lookup(labels, table):
    result = jnp.zeros(labels.shape, jnp.float32)
    for region in range(table.shape[0]):
        result = result + jnp.where(labels == region, table[region], 0.0)
    return result


def inner_products(left, right):
    return jnp.dot(
        left, right.T, precision=lax.Precision.HIGHEST, preferred_element_type=jnp.float32
    )


def apply_operator(padded_basis, coupling, permittivity, shift_scalar):
    columns = padded_basis.shape[0]
    blocks = padded_basis.reshape((columns // 16, 16) + padded_basis.shape[1:])

    def apply_block(column_block):
        return operator_block(column_block, coupling, permittivity, shift_scalar)

    images = lax.map(apply_block, blocks)
    return images.reshape((columns,) + images.shape[2:])


def factor_inverse(gram_matrix):
    lower_factor = jnp.linalg.cholesky(gram_matrix)
    inverse = lax.linalg.triangular_solve(
        lower_factor, jnp.eye(gram_matrix.shape[0], dtype=jnp.float32), left_side=True, lower=True
    )
    return (lower_factor.T, inverse)


def local(krylov_basis, regions, mu_table, eps_table, shift_value):
    columns = krylov_basis.shape[0]
    flattened = krylov_basis.reshape(columns, -1)
    total_rows = flattened.shape[1] * lax.axis_size("row") * lax.axis_size("col")
    cells_y = regions.shape[1]
    labels = regions + 1
    from_lower_row = shifted(labels, "row", 1)
    from_lower_col = shifted(labels[:, cells_y - 1 :], "col", 1)
    corner_zero = jnp.zeros((1, 1, labels.shape[2]), jnp.int32)
    top_layer = jnp.concatenate([corner_zero, from_lower_row], axis=1)
    rest_layers = jnp.concatenate([from_lower_col, labels], axis=1)
    padded_ids = jnp.concatenate([top_layer, rest_layers], axis=0)
    mu_extended = jnp.concatenate([jnp.zeros((1,), jnp.float32), mu_table])
    coupling = lookup(padded_ids, mu_extended)
    permittivity = lookup(regions, eps_table)
    shift_scalar = shift_value[0]
    padded_basis = padded(krylov_basis, (("row", 2), ("col", 3)), 1)
    image_basis = apply_operator(padded_basis, coupling, permittivity, shift_scalar)
    image_flat = image_basis.reshape(columns, -1)
    gram_matrix, raw_proj = lax.psum(
        (
            inner_products(flattened, flattened) / total_rows,
            inner_products(flattened, image_flat) / total_rows,
        ),
        ("row", "col"),
    )
    upper_factor, inverse = factor_inverse(gram_matrix)
    orthonormal = jnp.dot(
        inverse, flattened, precision=lax.Precision.HIGHEST, preferred_element_type=jnp.float32
    ).reshape(krylov_basis.shape)
    applied = jnp.dot(
        inverse, image_flat, precision=lax.Precision.HIGHEST, preferred_element_type=jnp.float32
    ).reshape(krylov_basis.shape)
    half_proj = jnp.dot(
        inverse, raw_proj, precision=lax.Precision.HIGHEST, preferred_element_type=jnp.float32
    )
    projected = inner_products(half_proj, inverse)
    return (orthonormal, upper_factor, applied, projected)


def solution(mesh):
    placed = (P("shift", None, "row", "col", None), P("row", "col", None), P(), P(), P("shift"))
    return jax.shard_map(
        local,
        mesh=mesh,
        in_specs=placed,
        out_specs=(
            P("shift", None, "row", "col", None),
            P("shift", None),
            P("shift", None, "row", "col", None),
            P("shift", None),
        ),
        check_vma=False,
    )
```

profile of v0, /device:TPU:0, one launch (start us, length us, event | category | flops | bytes accessed | tf_op | source)
XLA Modules:
  0.0 131.0 jit_solution(15011954159071276242)
XLA Ops:
  0.7 1.1 copy.27
  1.7 4.9 %collective-permute-start.2 = (f32[64,3,1,4,128]{4,0,3,2,1:T(8,128)S(1)}, f32[64,3,1,4,128]{4,0,3,2,1:T(8,128)S(1)}, u32[]{:S(2)}, u32[]{:S(2)}) collective-permute-start(f32[64,3,1,4,128]{4,0,3,2,1:T(8,128)S(1)} %copy.27), channel_id=1, source_target_pairs={{0,2},{2,4},{4,6},{6,8},{8,10},{10,12},{12,14},{1,3},{3,5},{5,7},{... | collective-permute-start | bytes 1179656 | tf_op jit(solution)/shard_map/ppermute | solution.py:20
  6.6 1.3 collective-permute-start.3
  8.6 4.5 %collective-permute-start = (s32[1,4,128]{2,1,0:T(4,128)S(1)}, s32[1,4,128]{2,1,0:T(4,128)S(1)}, u32[]{:S(2)}, u32[]{:S(2)}) collective-permute-start(s32[1,4,128]{2,1,0:T(4,128)S(1)} %broadcast_add_fusion), channel_id=1, source_target_pairs={{0,2},{2,4},{4,6},{6,8},{8,10},{10,12},{12,14},{1,3},{3,5},{5,7},{... | collective-permute-start | bytes 6152 | tf_op jit(solution)/shard_map/ppermute | solution.py:10
  13.2 1.3 collective-permute-start.1
  14.5 1.6 %fusion.16 = f32[64,64]{0,1:T(8,128)S(1)} fusion(f32[64,3,4,128]{3,2,1,0:T(4,128)} %bitcast.98), kind=kOutput, calls=%fused_computation.37 | convolution fusion | flops 75501568 | bytes 409600 | tf_op jit(solution)/shard_map/dot_general | solution.py:85
  16.8 6.7 %collective-permute-done.2 = f32[64,3,1,4,128]{4,0,3,2,1:T(8,128)S(1)} collective-permute-done((f32[64,3,1,4,128]{4,0,3,2,1:T(8,128)S(1)}, f32[64,3,1,4,128]{4,0,3,2,1:T(8,128)S(1)}, u32[]{:S(2)}, u32[]{:S(2)}) %collective-permute-start.2) | collective-permute-done | bytes 393248 | tf_op jit(solution)/shard_map/ppermute | solution.py:20
  23.6 1.3 collective-permute-start.4
  24.9 1.3 collective-permute-start.5
  26.2 5.1 %select_add_fusion.1 = f32[1,4,128]{2,1,0:T(4,128)S(1)} fusion(s32[1,4,128]{2,1,0:T(4,128)S(1)} %copy-done.5, f32[]{:T(128)} %bitcast.37, f32[]{:T(128)} %bitcast.36, f32[]{:T(128)} %bitcast.35, f32[]{:T(128)} %bitcast.34, f32[]{:T(128)} %bitcast.33, f32[]{:T(128)} %bitcast.32, f32[]{:T(128)} %bitcast.31, f32[]{:T(128)} %bitcast.30), kind=kLoop, calls=%fused_computation.58 | loop fusion | flops 11776 | bytes 4128 | tf_op jit(solution)/shard_map/add | solution.py:80
  32.2 0.9 reshape.59
  33.1 5.0 %select_add_fusion = f32[2,5,128]{2,1,0:T(8,128)S(1)} fusion(s32[1,4,128]{2,1,0:T(4,128)S(1)} %broadcast_add_fusion, s32[1,1,128]{2,1,0:T(1,128)S(1)} %collective-permute-done.1, s32[1,4,128]{2,1,0:T(4,128)S(1)} %collective-permute-done, f32[]{:T(128)} %bitcast.27, f32[]{:T(128)} %bitcast.26, f32[]{:T(128)} %bitcast.25, f32[]{:T(128)} %bitcast.24, ...), kind=kLoop, calls=%fused_computation.57 | loop fusion | flops 32000 | bytes 9760 | tf_op jit(solution)/shard_map/add | solution.py:80
  38.1 0.7 copy-done.2
  38.8 1.2 pad_maximum_fusion.1
  40.0 8.1 %while.12 = (s32[]{:T(128)}, f32[4,16,3,1,4,128]{5,4,3,2,1,0:T(4,128)}, f32[2,5,128]{2,1,0:T(8,128)S(1)}, f32[4,16,3,3,6,128]{5,1,0,4,3,2:T(8,128)S(1)}, f32[]{:T(128)}, /*index=5*/f32[1,4,128]{2,1,0:T(4,128)S(1)}, s32[]{:T(128)}) while((s32[]{:T(128)}, f32[4,16,3,1,4,128]{5,4,3,2,1,0:T(4,128)}, f32[2,5,128]{2,1,0:T(8,128)S(1)}, ...), condition=%wide.region_4.5_spmd, body=%wide.region_3.4_spmd.sunk | while | flops 418306 | bytes 4790613 | solution.py:97
  41.3 0.7 fusion.42
  48.1 1.2 reshape_reshape.3
  49.7 64.1 %all-reduce.5 = (f32[64,64]{0,1:T(8,128)S(1)}, f32[64,64]{1,0:T(8,128)S(1)}) all-reduce(f32[64,64]{0,1:T(8,128)S(1)} %fusion.16, f32[64,64]{1,0:T(8,128)S(1)} %fusion.15), channel_id=1, replica_groups=mesh['shift'=2,'row'=8,'col'=2] {'row','col'}, use_global_device_ids=true, to_apply=%region_0.1 | all-reduce | flops 8192 | bytes 65536 | tf_op jit(solution)/shard_map/psum | solution.py:128
  113.9 5.8 %cholesky.17 = f32[64,64]{1,0:T(8,128)S(1)} custom-call(f32[64,64]{1,0:T(8,128)S(1)} %fusion.24), custom_call_target="Cholesky" | custom-call | tf_op jit(solution)/shard_map/jit(cholesky)/cholesky | solution.py:102
  121.1 4.9 %custom-call.6 = f32[1,64,64]{1,2,0:T(8,128)S(1)} custom-call(f32[1,64,64]{2,1,0:T(8,128)S(1)} %get-tuple-element.122), custom_call_target="InvertDiagBlocksLowerTriangular" | custom-call | tf_op jit(solution)/shard_map/triangular_solve | solution.py:103
  126.4 0.8 fusion.30
  127.8 1.0 copy.34
  129.3 1.0 copy.32
  130.3 0.7 copy.33
  (80 shorter events, 12.9 us)
Async XLA Ops:
  0.6 22.8 %copy-start = (f32[64,3,1,4,128]{4,3,2,1,0:T(4,128)S(1)}, f32[64,3,1,4,128]{4,3,2,1,0:T(4,128)}, u32[]{:S(2)}) copy-start(f32[64,3,1,4,128]{4,3,2,1,0:T(4,128)} %param.7) | copy-start | bytes 1179652
  0.6 15.4 %copy-start.3 = (f32[8]{0:T(128)S(1)}, f32[8]{0:T(128)}, u32[]{:S(2)}) copy-start(f32[8]{0:T(128)} %param.10) | copy-start | bytes 100
  1.7 21.7 %collective-permute-start.2 = (f32[64,3,1,4,128]{4,0,3,2,1:T(8,128)S(1)}, f32[64,3,1,4,128]{4,0,3,2,1:T(8,128)S(1)}, u32[]{:S(2)}, u32[]{:S(2)}) collective-permute-start(f32[64,3,1,4,128]{4,0,3,2,1:T(8,128)S(1)} %copy.27), channel_id=1, source_target_pairs={{0,2},{2,4},{4,6},{6,8},{8,10},{10,12},{12,14},{1,3},{3,5},{5,7},{... | collective-permute-start | bytes 1179656 | tf_op jit(solution)/shard_map/ppermute | solution.py:20
  6.6 16.9 %collective-permute-start.3 = (f32[64,3,1,4,128]{4,0,3,2,1:T(8,128)S(1)}, f32[64,3,1,4,128]{4,0,3,2,1:T(8,128)S(1)}, u32[]{:S(2)}, u32[]{:S(2)}) collective-permute-start(f32[64,3,1,4,128]{4,0,3,2,1:T(8,128)S(1)} %copy.27), channel_id=1, source_target_pairs={{2,0},{4,2},{6,4},{8,6},{10,8},{12,10},{14,12},{3,1},{5,3},{7,5},{... | collective-permute-start | bytes 1179656 | tf_op jit(solution)/shard_map/ppermute | solution.py:21
  8.6 24.5 %collective-permute-start = (s32[1,4,128]{2,1,0:T(4,128)S(1)}, s32[1,4,128]{2,1,0:T(4,128)S(1)}, u32[]{:S(2)}, u32[]{:S(2)}) collective-permute-start(s32[1,4,128]{2,1,0:T(4,128)S(1)} %broadcast_add_fusion), channel_id=1, source_target_pairs={{0,2},{2,4},{4,6},{6,8},{8,10},{10,12},{12,14},{1,3},{3,5},{5,7},{... | collective-permute-start | bytes 6152 | tf_op jit(solution)/shard_map/ppermute | solution.py:10
  13.2 19.9 %collective-permute-start.1 = (s32[1,1,128]{2,1,0:T(1,128)S(1)}, s32[1,1,128]{2,1,0:T(1,128)S(1)}, u32[]{:S(2)}, u32[]{:S(2)}) collective-permute-start(s32[1,1,128]{2,1,0:T(1,128)S(1)} %slice.209), channel_id=1, source_target_pairs={{0,1},{2,3},{4,5},{6,7},{8,9},{10,11},{12,13},{14,15},{16,17},{18,... | collective-permute-start | bytes 1544 | tf_op jit(solution)/shard_map/ppermute | solution.py:10
  23.5 2.7 %copy-start.5 = (s32[1,4,128]{2,1,0:T(4,128)S(1)}, s32[1,4,128]{2,1,0:T(4,128)}, u32[]{:S(2)}) copy-start(s32[1,4,128]{2,1,0:T(4,128)} %param.8) | copy-start | bytes 6148
  23.5 7.8 %copy-start.4 = (f32[8]{0:T(128)S(1)}, f32[8]{0:T(128)}, u32[]{:S(2)}) copy-start(f32[8]{0:T(128)} %param.9) | copy-start | bytes 100
  23.6 14.5 %collective-permute-start.4 = (f32[64,3,3,1,128]{4,0,3,2,1:T(8,128)S(1)}, f32[64,3,3,1,128]{4,0,3,2,1:T(8,128)S(1)}, u32[]{:S(2)}, u32[]{:S(2)}) collective-permute-start(f32[64,3,3,1,128]{4,0,3,2,1:T(8,128)S(1)} %get-tuple-element.119), channel_id=1, source_target_pairs={{0,1},{2,3},{4,5},{6,7},{8,9},{10,11},{12,13},{14,15},{16,17},{18,... | collective-permute-start | bytes 884744 | tf_op jit(solution)/shard_map/ppermute | solution.py:20
  24.9 13.9 %collective-permute-start.5 = (f32[64,3,3,1,128]{4,0,3,2,1:T(8,128)S(1)}, f32[64,3,3,1,128]{4,0,3,2,1:T(8,128)}, u32[]{:S(2)}, u32[]{:S(2)}) collective-permute-start(f32[64,3,3,1,128]{4,0,3,2,1:T(8,128)S(1)} %get-tuple-element.120), channel_id=1, source_target_pairs={{1,0},{3,2},{5,4},{7,6},{9,8},{11,10},{13,12},{15,14},{17,16},{19,... | collective-permute-start | bytes 884744 | tf_op jit(solution)/shard_map/ppermute | solution.py:21
  38.1 0.7 copy-start.2
  127.2 1.6 %copy-start.1 = (f32[3,4,128,64]{2,1,0,3:T(4,128)S(1)}, f32[3,4,128,64]{2,1,0,3:T(4,128)}, u32[]{:S(2)}) copy-start(f32[3,4,128,64]{2,1,0,3:T(4,128)} %reshape.59) | copy-start | bytes 1179652
where the time goes:
time: 132 us; the launch traced here: 131 us
  blocking collectives  64.1 us (49%)
  other arithmetic  30.2 us (23%)
  starting transfers between devices  14.6 us (11%)
  local copies, waits for them, and re-layouts  10.1 us (8%)
  waiting for transfers between devices  6.67 us (5%)
  matrix products  4.19 us (3%)
    psum x1, blocking collectives, local(): lax.psum((inner_products(flattened, flattened) / total_rows, inner_produc...  64.1 us
    add x2, other arithmetic, lookup(): result = result + jnp.where(labels == region, table[region], 0.0)  10.1 us
    ppermute x2, waiting for transfers between devices, padded(): before = lax.ppermute(last, axis, up)  6.66 us
    another operation x3, other arithmetic, factor_inverse(): lower_factor = jnp.linalg.cholesky(gram_matrix)  6.52 us
    ppermute x2, starting transfers between devices, padded(): before = lax.ppermute(last, axis, up)  6.2 us
    ppermute x2, starting transfers between devices, shifted(): return lax.ppermute(x, axis, pairs)  5.82 us
    another operation x1, other arithmetic, factor_inverse(): lax.linalg.triangular_solve(lower_factor, jnp.eye(gram_matrix.shape[0], d...  4.9 us
    unnamed x18, local copies, waits for them, and re-layouts  4.56 us
  transfers between devices with their start and end apart: 6, of which 1 were waited for; matrix products, arithmetic and copies ran while one was open for 11% of the time, Pallas kernels for 0%

commit v1 on v0

--- a/solution.py
+++ b/solution.py
@@ -125,13 +125,13 @@
     padded_basis = padded(krylov_basis, (("row", 2), ("col", 3)), 1)
     image_basis = apply_operator(padded_basis, coupling, permittivity, shift_scalar)
     image_flat = image_basis.reshape(columns, -1)
-    gram_matrix, raw_proj = lax.psum(
-        (
+    partial = jnp.stack(
+        [
             inner_products(flattened, flattened) / total_rows,
             inner_products(flattened, image_flat) / total_rows,
-        ),
-        ("row", "col"),
+        ]
     )
+    gram_matrix, raw_proj = jnp.sum(lax.all_gather(partial, ("row", "col")), axis=0)
     upper_factor, inverse = factor_inverse(gram_matrix)
     orthonormal = jnp.dot(
         inverse, flattened, precision=lax.Precision.HIGHEST, preferred_element_type=jnp.float32

time: 132 us -> 89.2 us (0.68)
  blocking collectives: 64.1 us -> 26 us
  waiting for transfers between devices: 6.67 us -> 1.55 us
    psum x1 -> x0, blocking collectives: 64.1 us -> none  [local(): lax.psum((inner_products(flattened, flattened) / total_rows, inner_produc...]
    all_gather x0 -> x1, blocking collectives: none -> 26 us  [local(): lax.all_gather(partial, ('row', 'col'))]
    ppermute x2, waiting for transfers between devices: 6.66 us -> 1.53 us  [padded(): before = lax.ppermute(last, axis, up)]
    unnamed x18 -> x15, local copies, waits for them, and re-layouts: 4.56 us -> 4.63 us
  transfers between devices with their start and end apart: 6 -> 6, of which waited for: 1 -> 1; matrix products, arithmetic and copies ran while one was open for 11% -> 18% of each run, Pallas kernels for 0% -> 0%
where the time goes in v1:
time: 89.2 us; the launch traced here: 88.6 us
  other arithmetic  31.2 us (35%)
  blocking collectives  26 us (29%)
  starting transfers between devices  14.6 us (16%)
  local copies, waits for them, and re-layouts  11 us (12%)
  matrix products  3.05 us (3%)
  waiting for transfers between devices  1.55 us (2%)
    all_gather x1, blocking collectives, local(): lax.all_gather(partial, ('row', 'col'))  26 us
    add x2, other arithmetic, lookup(): result = result + jnp.where(labels == region, table[region], 0.0)  10.9 us
    another operation x3, other arithmetic, factor_inverse(): lower_factor = jnp.linalg.cholesky(gram_matrix)  6.52 us
    ppermute x2, starting transfers between devices, padded(): before = lax.ppermute(last, axis, up)  6.2 us
    ppermute x2, starting transfers between devices, shifted(): return lax.ppermute(x, axis, pairs)  5.82 us
    another operation x1, other arithmetic, factor_inverse(): lax.linalg.triangular_solve(lower_factor, jnp.eye(gram_matrix.shape[0], d...  4.9 us
    unnamed x15, local copies, waits for them, and re-layouts  4.63 us
    dynamic_update_slice x4, other arithmetic, apply_operator(): images = lax.map(apply_block, blocks)  2.76 us
  transfers between devices with their start and end apart: 6, of which 1 were waited for; matrix products, arithmetic and copies ran while one was open for 18% of the time, Pallas kernels for 0%

profile of v1, /device:TPU:0, one launch (start us, length us, event | category | flops | bytes accessed | tf_op | source)
XLA Modules:
  0.0 88.6 jit_solution(7166668178619069719)
XLA Ops:
  0.6 1.1 %copy.43 = f32[64,3,1,4,128]{4,0,3,2,1:T(8,128)S(1)} copy(f32[64,3,1,4,128]{4,3,2,1,0:T(4,128)} %param.7) | data formatting | bytes 786432 | tf_op args[0]
  1.7 4.9 %collective-permute-start.2 = (f32[64,3,1,4,128]{4,0,3,2,1:T(8,128)S(1)}, f32[64,3,1,4,128]{4,0,3,2,1:T(8,128)S(1)}, u32[]{:S(2)}, u32[]{:S(2)}) collective-permute-start(f32[64,3,1,4,128]{4,0,3,2,1:T(8,128)S(1)} %copy.43), channel_id=1, source_target_pairs={{0,2},{2,4},{4,6},{6,8},{8,10},{10,12},{12,14},{1,3},{3,5},{5,7},{... | collective-permute-start | bytes 1179656 | tf_op jit(solution)/shard_map/ppermute | solution.py:20
  6.6 1.3 %collective-permute-start.3 = (f32[64,3,1,4,128]{4,0,3,2,1:T(8,128)S(1)}, f32[64,3,1,4,128]{4,0,3,2,1:T(8,128)S(1)}, u32[]{:S(2)}, u32[]{:S(2)}) collective-permute-start(f32[64,3,1,4,128]{4,0,3,2,1:T(8,128)S(1)} %copy.43), channel_id=1, source_target_pairs={{2,0},{4,2},{6,4},{8,6},{10,8},{12,10},{14,12},{3,1},{5,3},{7,5},{... | collective-permute-start | bytes 1179656 | tf_op jit(solution)/shard_map/ppermute | solution.py:21
  8.6 4.5 %collective-permute-start = (s32[1,4,128]{2,1,0:T(4,128)S(1)}, s32[1,4,128]{2,1,0:T(4,128)S(1)}, u32[]{:S(2)}, u32[]{:S(2)}) collective-permute-start(s32[1,4,128]{2,1,0:T(4,128)S(1)} %broadcast_add_fusion), channel_id=1, source_target_pairs={{0,2},{2,4},{4,6},{6,8},{8,10},{10,12},{12,14},{1,3},{3,5},{5,7},{... | collective-permute-start | bytes 6152 | tf_op jit(solution)/shard_map/ppermute | solution.py:10
  13.2 1.3 %collective-permute-start.1 = (s32[1,1,128]{2,1,0:T(1,128)S(1)}, s32[1,1,128]{2,1,0:T(1,128)S(1)}, u32[]{:S(2)}, u32[]{:S(2)}) collective-permute-start(s32[1,1,128]{2,1,0:T(1,128)S(1)} %slice.209), channel_id=1, source_target_pairs={{0,1},{2,3},{4,5},{6,7},{8,9},{10,11},{12,13},{14,15},{16,17},{18,... | collective-permute-start | bytes 1544 | tf_op jit(solution)/shard_map/ppermute | solution.py:10
  14.5 1.6 %fusion.29 = (f32[1]{0:T(128)}, f32[1]{0:T(128)}, f32[1]{0:T(128)}, f32[1]{0:T(128)}, f32[1]{0:T(128)}, /*index=5*/f32[1]{0:T(128)}, f32[1]{0:T(128)}, f32[1]{0:T(128)}) fusion(f32[8]{0:T(128)} %param.10), kind=kLoop, calls=%fused_computation.66 | loop fusion | bytes 64 | tf_op jit(solution)/shard_map/slice | solution.py:80
  16.1 5.8 %select_add_fusion.1 = f32[1,4,128]{2,1,0:T(4,128)S(1)} fusion(s32[1,4,128]{2,1,0:T(4,128)} %param.8, f32[]{:T(128)} %bitcast.30, f32[]{:T(128)} %bitcast.29, f32[]{:T(128)} %bitcast.28, f32[]{:T(128)} %bitcast.27, f32[]{:T(128)} %bitcast.26, f32[]{:T(128)} %bitcast.25, f32[]{:T(128)} %bitcast.24, f32[]{:T(128)} %bitcast.23), kind=kLoop, calls=%fused_computation.62 | loop fusion | flops 11776 | bytes 4128 | tf_op jit(solution)/shard_map/add | solution.py:80
  21.9 1.5 %collective-permute-done.2 = f32[64,3,1,4,128]{4,0,3,2,1:T(8,128)S(1)} collective-permute-done((f32[64,3,1,4,128]{4,0,3,2,1:T(8,128)S(1)}, f32[64,3,1,4,128]{4,0,3,2,1:T(8,128)S(1)}, u32[]{:S(2)}, u32[]{:S(2)}) %collective-permute-start.2) | collective-permute-done | bytes 393248 | tf_op jit(solution)/shard_map/ppermute | solution.py:20
  23.6 1.3 %collective-permute-start.4 = (f32[64,3,3,1,128]{4,0,3,2,1:T(8,128)S(1)}, f32[64,3,3,1,128]{4,0,3,2,1:T(8,128)S(1)}, u32[]{:S(2)}, u32[]{:S(2)}) collective-permute-start(f32[64,3,3,1,128]{4,0,3,2,1:T(8,128)S(1)} %get-tuple-element.127), channel_id=1, source_target_pairs={{0,1},{2,3},{4,5},{6,7},{8,9},{10,11},{12,13},{14,15},{16,17},{18,... | collective-permute-start | bytes 884744 | tf_op jit(solution)/shard_map/ppermute | solution.py:20
  24.9 1.3 %collective-permute-start.5 = (f32[64,3,3,1,128]{4,0,3,2,1:T(8,128)S(1)}, f32[64,3,3,1,128]{4,0,3,2,1:T(8,128)}, u32[]{:S(2)}, u32[]{:S(2)}) collective-permute-start(f32[64,3,3,1,128]{4,0,3,2,1:T(8,128)S(1)} %get-tuple-element.128), channel_id=1, source_target_pairs={{1,0},{3,2},{5,4},{7,6},{9,8},{11,10},{13,12},{15,14},{17,16},{19,... | collective-permute-start | bytes 884744 | tf_op jit(solution)/shard_map/ppermute | solution.py:21
  27.5 0.9 reshape.60
  28.4 5.2 %select_add_fusion = f32[2,5,128]{2,1,0:T(8,128)S(1)} fusion(s32[1,4,128]{2,1,0:T(4,128)S(1)} %broadcast_add_fusion, s32[1,1,128]{2,1,0:T(1,128)S(1)} %collective-permute-done.1, s32[1,4,128]{2,1,0:T(4,128)S(1)} %collective-permute-done, f32[]{:T(128)} %bitcast.20, f32[]{:T(128)} %bitcast.19, f32[]{:T(128)} %bitcast.18, f32[]{:T(128)} %bitcast.17, ...), kind=kLoop, calls=%fused_computation.61 | loop fusion | flops 32000 | bytes 9760 | tf_op jit(solution)/shard_map/add | solution.py:80
  33.6 0.7 copy-done.2
  34.3 1.2 %pad_maximum_fusion.1 = f32[64,3,3,6,128]{4,0,3,2,1:T(8,128)S(1)} fusion(f32[64,3,3,1,128]{4,0,3,2,1:T(8,128)} %collective-permute-done.5, f32[64,3,3,4,128]{4,0,3,2,1:T(8,128)S(1)} %constant_dynamic-update-slice_fusion, f32[64,3,3,1,128]{4,0,3,2,1:T(8,128)} %copy-done.2), kind=kLoop, calls=%fused_computation.31 | loop fusion | flops 884736 | bytes 3538944 | tf_op jit(solution)/shard_map/concatenate | solution.py:22
  35.5 8.1 %while.12 = (s32[]{:T(128)}, f32[4,16,3,1,4,128]{5,4,3,2,1,0:T(4,128)}, f32[2,5,128]{2,1,0:T(8,128)S(1)}, f32[4,16,3,3,6,128]{5,1,0,4,3,2:T(8,128)S(1)}, f32[]{:T(128)}, /*index=5*/f32[1,4,128]{2,1,0:T(4,128)S(1)}, s32[]{:T(128)}) while((s32[]{:T(128)}, f32[4,16,3,1,4,128]{5,4,3,2,1,0:T(4,128)}, f32[2,5,128]{2,1,0:T(8,128)S(1)}, ...), condition=%wide.region_1.2_spmd, body=%wide.region_0.1_spmd.sunk | while | flops 418306 | bytes 4790613 | solution.py:97
  36.9 0.7 fusion.42
  43.7 1.2 %reshape_reshape.3 = f32[64,1536]{1,0:T(8,128)S(1)} reshape(f32[4,16,3,1,4,128]{5,4,3,2,1,0:T(4,128)} %get-tuple-element.81) | data formatting | bytes 786432 | tf_op jit(solution)/shard_map/reshape;reshape | solution.py:127
  45.3 26.0 %all-gather = f32[32,64,64]{2,1,0:T(8,128)S(1)} all-gather(f32[2,64,64]{2,1,0:T(8,128)S(1)} %pad_maximum_fusion.2), channel_id=2, replica_groups=mesh['shift'=2,'row'=8,'col'=2] {'row','col'}, dimensions={0}, use_global_device_ids=true | all-gather | bytes 557056 | tf_op jit(solution)/shard_map/all_gather | solution.py:134
  71.5 5.8 %cholesky.17 = f32[64,64]{1,0:T(8,128)S(1)} custom-call(f32[64,64]{1,0:T(8,128)S(1)} %fusion.22), custom_call_target="Cholesky" | custom-call | tf_op jit(solution)/shard_map/jit(cholesky)/cholesky | solution.py:102
  78.7 4.9 %custom-call.6 = f32[1,64,64]{1,2,0:T(8,128)S(1)} custom-call(f32[1,64,64]{2,1,0:T(8,128)S(1)} %get-tuple-element.130), custom_call_target="InvertDiagBlocksLowerTriangular" | custom-call | tf_op jit(solution)/shard_map/triangular_solve | solution.py:103
  84.0 0.8 fusion.31
  85.4 1.0 %copy.54 = f32[64,3,1,4,128]{4,3,2,1,0:T(4,128)} copy(f32[64,3,1,4,128]{4,0,3,1,2:T(8,128)S(1)} %convolution_bitcast_fusion) | data formatting | bytes 786432
  86.9 1.0 %copy.52 = f32[64,3,1,4,128]{4,3,2,1,0:T(4,128)} copy(f32[64,3,1,4,128]{4,0,3,1,2:T(8,128)S(1)} %convolution_bitcast_fusion.1) | data formatting | bytes 786432
  87.9 0.7 copy.53
  (79 shorter events, 12.7 us)
Async XLA Ops:
  0.6 22.8 %copy-start = (f32[64,3,1,4,128]{4,3,2,1,0:T(4,128)S(1)}, f32[64,3,1,4,128]{4,3,2,1,0:T(4,128)}, u32[]{:S(2)}) copy-start(f32[64,3,1,4,128]{4,3,2,1,0:T(4,128)} %param.7) | copy-start | bytes 1179652
  1.7 21.7 %collective-permute-start.2 = (f32[64,3,1,4,128]{4,0,3,2,1:T(8,128)S(1)}, f32[64,3,1,4,128]{4,0,3,2,1:T(8,128)S(1)}, u32[]{:S(2)}, u32[]{:S(2)}) collective-permute-start(f32[64,3,1,4,128]{4,0,3,2,1:T(8,128)S(1)} %copy.43), channel_id=1, source_target_pairs={{0,2},{2,4},{4,6},{6,8},{8,10},{10,12},{12,14},{1,3},{3,5},{5,7},{... | collective-permute-start | bytes 1179656 | tf_op jit(solution)/shard_map/ppermute | solution.py:20
  6.6 16.9 %collective-permute-start.3 = (f32[64,3,1,4,128]{4,0,3,2,1:T(8,128)S(1)}, f32[64,3,1,4,128]{4,0,3,2,1:T(8,128)S(1)}, u32[]{:S(2)}, u32[]{:S(2)}) collective-permute-start(f32[64,3,1,4,128]{4,0,3,2,1:T(8,128)S(1)} %copy.43), channel_id=1, source_target_pairs={{2,0},{4,2},{6,4},{8,6},{10,8},{12,10},{14,12},{3,1},{5,3},{7,5},{... | collective-permute-start | bytes 1179656 | tf_op jit(solution)/shard_map/ppermute | solution.py:21
  8.6 19.8 %collective-permute-start = (s32[1,4,128]{2,1,0:T(4,128)S(1)}, s32[1,4,128]{2,1,0:T(4,128)S(1)}, u32[]{:S(2)}, u32[]{:S(2)}) collective-permute-start(s32[1,4,128]{2,1,0:T(4,128)S(1)} %broadcast_add_fusion), channel_id=1, source_target_pairs={{0,2},{2,4},{4,6},{6,8},{8,10},{10,12},{12,14},{1,3},{3,5},{5,7},{... | collective-permute-start | bytes 6152 | tf_op jit(solution)/shard_map/ppermute | solution.py:10
  13.2 15.2 %collective-permute-start.1 = (s32[1,1,128]{2,1,0:T(1,128)S(1)}, s32[1,1,128]{2,1,0:T(1,128)S(1)}, u32[]{:S(2)}, u32[]{:S(2)}) collective-permute-start(s32[1,1,128]{2,1,0:T(1,128)S(1)} %slice.209), channel_id=1, source_target_pairs={{0,1},{2,3},{4,5},{6,7},{8,9},{10,11},{12,13},{14,15},{16,17},{18,... | collective-permute-start | bytes 1544 | tf_op jit(solution)/shard_map/ppermute | solution.py:10
  23.5 3.2 %copy-start.3 = (f32[8]{0:T(128)S(1)}, f32[8]{0:T(128)}, u32[]{:S(2)}) copy-start(f32[8]{0:T(128)} %param.9) | copy-start | bytes 100
  23.6 10.0 %collective-permute-start.4 = (f32[64,3,3,1,128]{4,0,3,2,1:T(8,128)S(1)}, f32[64,3,3,1,128]{4,0,3,2,1:T(8,128)S(1)}, u32[]{:S(2)}, u32[]{:S(2)}) collective-permute-start(f32[64,3,3,1,128]{4,0,3,2,1:T(8,128)S(1)} %get-tuple-element.127), channel_id=1, source_target_pairs={{0,1},{2,3},{4,5},{6,7},{8,9},{10,11},{12,13},{14,15},{16,17},{18,... | collective-permute-start | bytes 884744 | tf_op jit(solution)/shard_map/ppermute | solution.py:20
  24.9 9.4 %collective-permute-start.5 = (f32[64,3,3,1,128]{4,0,3,2,1:T(8,128)S(1)}, f32[64,3,3,1,128]{4,0,3,2,1:T(8,128)}, u32[]{:S(2)}, u32[]{:S(2)}) collective-permute-start(f32[64,3,3,1,128]{4,0,3,2,1:T(8,128)S(1)} %get-tuple-element.128), channel_id=1, source_target_pairs={{1,0},{3,2},{5,4},{7,6},{9,8},{11,10},{13,12},{15,14},{17,16},{19,... | collective-permute-start | bytes 884744 | tf_op jit(solution)/shard_map/ppermute | solution.py:21
  33.6 0.7 copy-start.2
  84.8 1.6 %copy-start.1 = (f32[3,4,128,64]{2,1,0,3:T(4,128)S(1)}, f32[3,4,128,64]{2,1,0,3:T(4,128)}, u32[]{:S(2)}) copy-start(f32[3,4,128,64]{2,1,0,3:T(4,128)} %reshape.60) | copy-start | bytes 1179652

commit v2 on v1

--- a/solution.py
+++ b/solution.py
@@ -75,10 +75,9 @@
 
 
 def lookup(labels, table):
-    result = jnp.zeros(labels.shape, jnp.float32)
-    for region in range(table.shape[0]):
-        result = result + jnp.where(labels == region, table[region], 0.0)
-    return result
+    regions = jnp.arange(table.shape[0], dtype=labels.dtype)
+    chosen = jnp.where(labels[..., None] == regions, table, 0.0)
+    return jnp.sum(chosen, axis=-1)
 
 
 def inner_products(left, right):
@@ -111,19 +110,17 @@
     flattened = krylov_basis.reshape(columns, -1)
     total_rows = flattened.shape[1] * lax.axis_size("row") * lax.axis_size("col")
     cells_y = regions.shape[1]
-    labels = regions + 1
-    from_lower_row = shifted(labels, "row", 1)
-    from_lower_col = shifted(labels[:, cells_y - 1 :], "col", 1)
-    corner_zero = jnp.zeros((1, 1, labels.shape[2]), jnp.int32)
+    local_mu = lookup(regions, mu_table)
+    from_lower_row = shifted(local_mu, "row", 1)
+    from_lower_col = shifted(local_mu[:, cells_y - 1 :], "col", 1)
+    corner_zero = jnp.zeros((1, 1, local_mu.shape[2]), jnp.float32)
     top_layer = jnp.concatenate([corner_zero, from_lower_row], axis=1)
-    rest_layers = jnp.concatenate([from_lower_col, labels], axis=1)
-    padded_ids = jnp.concatenate([top_layer, rest_layers], axis=0)
-    mu_extended = jnp.concatenate([jnp.zeros((1,), jnp.float32), mu_table])
-    coupling = lookup(padded_ids, mu_extended)
+    rest_layers = jnp.concatenate([from_lower_col, local_mu], axis=1)
+    coupling = jnp.concatenate([top_layer, rest_layers], axis=0)
     permittivity = lookup(regions, eps_table)
     shift_scalar = shift_value[0]
     padded_basis = padded(krylov_basis, (("row", 2), ("col", 3)), 1)
-    image_basis = apply_operator(padded_basis, coupling, permittivity, shift_scalar)
+    image_basis = operator_block(padded_basis, coupling, permittivity, shift_scalar)
     image_flat = image_basis.reshape(columns, -1)
     partial = jnp.stack(
         [

time: 89.2 us -> 73.2 us (0.82)
  other arithmetic: 31.2 us -> 13.6 us
  waiting for transfers between devices: 1.55 us -> 8.45 us
  local copies, waits for them, and re-layouts: 11 us -> 5.87 us
    add x3 -> x0, other arithmetic: 11.6 us -> none  [the longest x2 10.9 us: lookup(): result = result + jnp.where(labels == region, table[region], 0.0)]
    ppermute x2, waiting for transfers between devices: 1.53 us -> 7.71 us  [padded(): before = lax.ppermute(last, axis, up)]
    dynamic_update_slice x4 -> x0, other arithmetic: 2.76 us -> none  [apply_operator(): images = lax.map(apply_block, blocks)]
    mul x4 -> x1, other arithmetic: 2.6 us -> 0.01 us  [operator_block(): return stacked - shift_scalar * permittivity * interior]
    another operation x3 -> x2, local copies, waits for them, and re-layouts: 2.16 us -> 0.27 us  [the longest x1 1.15 us: local(): image_flat = image_basis.reshape(columns, -1)]
    slice x3 -> x1, local copies, waits for them, and re-layouts: 2.3 us -> 0.51 us  [local(): from_lower_col = shifted(local_mu[:, cells_y - 1:], 'col', 1)]
    concatenate x1, other arithmetic: 1.22 us -> 0.11 us  [padded(): x = jnp.concatenate([before, x, after], axis=dim)]
    unnamed x15 -> x11, local copies, waits for them, and re-layouts: 4.63 us -> 3.93 us
  transfers between devices with their start and end apart: 6 -> 6, of which waited for: 1 -> 2; matrix products, arithmetic and copies ran while one was open for 18% -> 4% of each run, Pallas kernels for 0% -> 0%
where the time goes in v2:
time: 73.2 us; the launch traced here: 72.9 us
  blocking collectives  25.2 us (34%)
  starting transfers between devices  14.6 us (20%)
  other arithmetic  13.6 us (19%)
  waiting for transfers between devices  8.45 us (12%)
  local copies, waits for them, and re-layouts  5.87 us (8%)
  matrix products  3.67 us (5%)
  between operations  1.62 us (2%)
    all_gather x1, blocking collectives, local(): lax.all_gather(partial, ('row', 'col'))  25.2 us
    ppermute x2, waiting for transfers between devices, padded(): before = lax.ppermute(last, axis, up)  7.71 us
    another operation x3, other arithmetic, factor_inverse(): lower_factor = jnp.linalg.cholesky(gram_matrix)  6.52 us
    ppermute x2, starting transfers between devices, padded(): before = lax.ppermute(last, axis, up)  6.2 us
    ppermute x2, starting transfers between devices, shifted(): return lax.ppermute(x, axis, pairs)  5.82 us
    another operation x1, other arithmetic, factor_inverse(): lax.linalg.triangular_solve(lower_factor, jnp.eye(gram_matrix.shape[0], d...  4.9 us
    unnamed x11, local copies, waits for them, and re-layouts  3.93 us
    ppermute x2, starting transfers between devices, padded(): after = lax.ppermute(leading, axis, down)  2.58 us
  transfers between devices with their start and end apart: 6, of which 2 were waited for; matrix products, arithmetic and copies ran while one was open for 4% of the time, Pallas kernels for 0%

profile of v2, /device:TPU:0, one launch (start us, length us, event | category | flops | bytes accessed | tf_op | source)
XLA Modules:
  0.0 72.9 jit_solution(9621926167236737158)
XLA Ops:
  0.6 1.1 %copy.76 = f32[64,3,1,4,128]{4,0,3,2,1:T(8,128)S(1)} copy(f32[64,3,1,4,128]{4,3,2,1,0:T(4,128)} %param.5) | data formatting | bytes 786432 | tf_op args[0]
  1.7 4.9 %collective-permute-start.2 = (f32[64,3,1,4,128]{4,0,3,2,1:T(8,128)S(1)}, f32[64,3,1,4,128]{4,0,3,2,1:T(8,128)S(1)}, u32[]{:S(2)}, u32[]{:S(2)}) collective-permute-start(f32[64,3,1,4,128]{4,0,3,2,1:T(8,128)S(1)} %copy.76), channel_id=1, source_target_pairs={{0,2},{2,4},{4,6},{6,8},{8,10},{10,12},{12,14},{1,3},{3,5},{5,7},{... | collective-permute-start | bytes 1179656 | tf_op jit(solution)/shard_map/ppermute | solution.py:20
  6.6 1.3 %collective-permute-start.3 = (f32[64,3,1,4,128]{4,0,3,2,1:T(8,128)S(1)}, f32[64,3,1,4,128]{4,0,3,2,1:T(8,128)S(1)}, u32[]{:S(2)}, u32[]{:S(2)}) collective-permute-start(f32[64,3,1,4,128]{4,0,3,2,1:T(8,128)S(1)} %copy.76), channel_id=1, source_target_pairs={{2,0},{4,2},{6,4},{8,6},{10,8},{12,10},{14,12},{3,1},{5,3},{7,5},{... | collective-permute-start | bytes 1179656 | tf_op jit(solution)/shard_map/ppermute | solution.py:21
  7.9 0.8 %select_reduce_fusion.1 = (f32[4,128]{1,0:T(4,128)S(1)}, f32[4,128]{1,0:T(4,128)S(1)}) fusion(f32[8]{0:T(128)} %param.8, s32[4,128]{1,0:T(4,128)} %bitcast.89, f32[8]{0:T(128)} %param.7), kind=kLoop, calls=%fused_computation.53 | loop fusion | flops 19456 | bytes 6208 | tf_op jit(solution)/shard_map/reduce_sum | solution.py:80
  8.7 4.5 %collective-permute-start = (f32[1,4,128]{2,1,0:T(4,128)S(1)}, f32[1,4,128]{2,1,0:T(4,128)S(1)}, u32[]{:S(2)}, u32[]{:S(2)}) collective-permute-start(f32[1,4,128]{2,1,0:T(4,128)S(1)} %bitcast.86), channel_id=1, source_target_pairs={{0,2},{2,4},{4,6},{6,8},{8,10},{10,12},{12,14},{1,3},{3,5},{5,7},{... | collective-permute-start | bytes 6152 | tf_op jit(solution)/shard_map/ppermute | solution.py:10
  13.3 0.5 slice.92
  13.8 1.3 %collective-permute-start.1 = (f32[1,1,128]{2,1,0:T(1,128)}, f32[1,1,128]{2,1,0:T(1,128)S(1)}, u32[]{:S(2)}, u32[]{:S(2)}) collective-permute-start(f32[1,1,128]{2,1,0:T(1,128)} %slice.92), channel_id=1, source_target_pairs={{0,1},{2,3},{4,5},{6,7},{8,9},{10,11},{12,13},{14,15},{16,17},{18,... | collective-permute-start | bytes 1544 | tf_op jit(solution)/shard_map/ppermute | solution.py:10
  15.7 7.7 %collective-permute-done.2 = f32[64,3,1,4,128]{4,0,3,2,1:T(8,128)S(1)} collective-permute-done((f32[64,3,1,4,128]{4,0,3,2,1:T(8,128)S(1)}, f32[64,3,1,4,128]{4,0,3,2,1:T(8,128)S(1)}, u32[]{:S(2)}, u32[]{:S(2)}) %collective-permute-start.2) | collective-permute-done | bytes 393248 | tf_op jit(solution)/shard_map/ppermute | solution.py:20
  23.6 1.3 %collective-permute-start.4 = (f32[64,3,3,1,128]{4,0,3,2,1:T(8,128)S(1)}, f32[64,3,3,1,128]{4,0,3,2,1:T(8,128)S(1)}, u32[]{:S(2)}, u32[]{:S(2)}) collective-permute-start(f32[64,3,3,1,128]{4,0,3,2,1:T(8,128)S(1)} %get-tuple-element.25), channel_id=1, source_target_pairs={{0,1},{2,3},{4,5},{6,7},{8,9},{10,11},{12,13},{14,15},{16,17},{18,... | collective-permute-start | bytes 884744 | tf_op jit(solution)/shard_map/ppermute | solution.py:20
  24.9 1.3 %collective-permute-start.5 = (f32[64,3,3,1,128]{4,0,3,2,1:T(8,128)S(1)}, f32[64,3,3,1,128]{4,0,3,2,1:T(8,128)S(1)}, u32[]{:S(2)}, u32[]{:S(2)}) collective-permute-start(f32[64,3,3,1,128]{4,0,3,2,1:T(8,128)S(1)} %get-tuple-element.26), channel_id=1, source_target_pairs={{1,0},{3,2},{5,4},{7,6},{9,8},{11,10},{13,12},{15,14},{17,16},{19,... | collective-permute-start | bytes 884744 | tf_op jit(solution)/shard_map/ppermute | solution.py:21
  26.2 1.1 %fusion.3 = f32[1,64,64]{2,1,0:T(8,128)} fusion(f32[64,3,4,128]{3,2,1,0:T(4,128)S(1)} %bitcast.81), kind=kOutput, calls=%fused_computation.8 | convolution fusion | flops 75501568 | bytes 409600 | tf_op jit(solution)/shard_map/dot_general | solution.py:84
  27.7 0.7 %collective-permute-done.5 = f32[64,3,3,1,128]{4,0,3,2,1:T(8,128)S(1)} collective-permute-done((f32[64,3,3,1,128]{4,0,3,2,1:T(8,128)S(1)}, f32[64,3,3,1,128]{4,0,3,2,1:T(8,128)S(1)}, u32[]{:S(2)}, u32[]{:S(2)}) %collective-permute-start.5) | collective-permute-done | bytes 294944 | tf_op jit(solution)/shard_map/ppermute | solution.py:21
  29.6 0.5 fusion.1
  30.3 25.2 %all-gather = f32[32,64,64]{2,1,0:T(8,128)S(1)} all-gather(f32[2,64,64]{2,1,0:T(8,128)S(1)} %pad_maximum_fusion.1), channel_id=2, replica_groups=mesh['shift'=2,'row'=8,'col'=2] {'row','col'}, dimensions={0}, use_global_device_ids=true | all-gather | bytes 557056 | tf_op jit(solution)/shard_map/all_gather | solution.py:131
  55.7 5.8 %cholesky.17 = f32[64,64]{1,0:T(8,128)S(1)} custom-call(f32[64,64]{1,0:T(8,128)S(1)} %fusion.22), custom_call_target="Cholesky" | custom-call | tf_op jit(solution)/shard_map/jit(cholesky)/cholesky | solution.py:101
  61.6 0.6 compare_reduce_fusion
  62.2 0.7 fusion.27
  62.9 4.9 %custom-call.6 = f32[1,64,64]{1,2,0:T(8,128)S(1)} custom-call(f32[1,64,64]{2,1,0:T(8,128)S(1)} %get-tuple-element.34), custom_call_target="InvertDiagBlocksLowerTriangular" | custom-call | tf_op jit(solution)/shard_map/triangular_solve | solution.py:102
  68.2 0.8 %fusion.29 = f32[64,64]{1,0:T(8,128)} fusion(f32[64,64]{1,0:T(8,128)S(1)} %fusion.21, f32[64,64]{1,0:T(8,128)S(1)} %fusion.25), kind=kOutput, calls=%fused_computation.64 | convolution fusion | flops 3145728 | bytes 49152 | tf_op jit(solution)/shard_map/dot_general | solution.py:84
  69.3 0.5 convolution_bitcast_fusion
  69.8 1.0 %copy.89 = f32[64,3,1,4,128]{4,3,2,1,0:T(4,128)} copy(f32[64,3,1,4,128]{4,0,3,1,2:T(8,128)S(1)} %convolution_bitcast_fusion) | data formatting | bytes 786432
  70.8 0.5 convolution_bitcast_fusion.1
  71.2 1.0 %copy.87 = f32[64,3,1,4,128]{4,3,2,1,0:T(4,128)} copy(f32[64,3,1,4,128]{4,0,3,1,2:T(8,128)S(1)} %convolution_bitcast_fusion.1) | data formatting | bytes 786432
  72.2 0.7 copy.88
  (36 shorter events, 2.7 us)
Async XLA Ops:
  0.6 22.8 %copy-start = (f32[64,3,1,4,128]{4,3,2,1,0:T(4,128)S(1)}, f32[64,3,1,4,128]{4,3,2,1,0:T(4,128)}, u32[]{:S(2)}) copy-start(f32[64,3,1,4,128]{4,3,2,1,0:T(4,128)} %param.5) | copy-start | bytes 1179652
  1.7 21.7 %collective-permute-start.2 = (f32[64,3,1,4,128]{4,0,3,2,1:T(8,128)S(1)}, f32[64,3,1,4,128]{4,0,3,2,1:T(8,128)S(1)}, u32[]{:S(2)}, u32[]{:S(2)}) collective-permute-start(f32[64,3,1,4,128]{4,0,3,2,1:T(8,128)S(1)} %copy.76), channel_id=1, source_target_pairs={{0,2},{2,4},{4,6},{6,8},{8,10},{10,12},{12,14},{1,3},{3,5},{5,7},{... | collective-permute-start | bytes 1179656 | tf_op jit(solution)/shard_map/ppermute | solution.py:20
  6.6 16.9 %collective-permute-start.3 = (f32[64,3,1,4,128]{4,0,3,2,1:T(8,128)S(1)}, f32[64,3,1,4,128]{4,0,3,2,1:T(8,128)S(1)}, u32[]{:S(2)}, u32[]{:S(2)}) collective-permute-start(f32[64,3,1,4,128]{4,0,3,2,1:T(8,128)S(1)} %copy.76), channel_id=1, source_target_pairs={{2,0},{4,2},{6,4},{8,6},{10,8},{12,10},{14,12},{3,1},{5,3},{7,5},{... | collective-permute-start | bytes 1179656 | tf_op jit(solution)/shard_map/ppermute | solution.py:21
  8.7 18.9 %collective-permute-start = (f32[1,4,128]{2,1,0:T(4,128)S(1)}, f32[1,4,128]{2,1,0:T(4,128)S(1)}, u32[]{:S(2)}, u32[]{:S(2)}) collective-permute-start(f32[1,4,128]{2,1,0:T(4,128)S(1)} %bitcast.86), channel_id=1, source_target_pairs={{0,2},{2,4},{4,6},{6,8},{8,10},{10,12},{12,14},{1,3},{3,5},{5,7},{... | collective-permute-start | bytes 6152 | tf_op jit(solution)/shard_map/ppermute | solution.py:10
  13.8 13.8 %collective-permute-start.1 = (f32[1,1,128]{2,1,0:T(1,128)}, f32[1,1,128]{2,1,0:T(1,128)S(1)}, u32[]{:S(2)}, u32[]{:S(2)}) collective-permute-start(f32[1,1,128]{2,1,0:T(1,128)} %slice.92), channel_id=1, source_target_pairs={{0,1},{2,3},{4,5},{6,7},{8,9},{10,11},{12,13},{14,15},{16,17},{18,... | collective-permute-start | bytes 1544 | tf_op jit(solution)/shard_map/ppermute | solution.py:10
  23.6 4.1 %collective-permute-start.4 = (f32[64,3,3,1,128]{4,0,3,2,1:T(8,128)S(1)}, f32[64,3,3,1,128]{4,0,3,2,1:T(8,128)S(1)}, u32[]{:S(2)}, u32[]{:S(2)}) collective-permute-start(f32[64,3,3,1,128]{4,0,3,2,1:T(8,128)S(1)} %get-tuple-element.25), channel_id=1, source_target_pairs={{0,1},{2,3},{4,5},{6,7},{8,9},{10,11},{12,13},{14,15},{16,17},{18,... | collective-permute-start | bytes 884744 | tf_op jit(solution)/shard_map/ppermute | solution.py:20
  24.9 3.5 %collective-permute-start.5 = (f32[64,3,3,1,128]{4,0,3,2,1:T(8,128)S(1)}, f32[64,3,3,1,128]{4,0,3,2,1:T(8,128)S(1)}, u32[]{:S(2)}, u32[]{:S(2)}) collective-permute-start(f32[64,3,3,1,128]{4,0,3,2,1:T(8,128)S(1)} %get-tuple-element.26), channel_id=1, source_target_pairs={{1,0},{3,2},{5,4},{7,6},{9,8},{11,10},{13,12},{15,14},{17,16},{19,... | collective-permute-start | bytes 884744 | tf_op jit(solution)/shard_map/ppermute | solution.py:21
  29.5 0.8 %copy-start.1 = (f32[1,64,64]{2,1,0:T(8,128)S(1)}, f32[1,64,64]{2,1,0:T(8,128)}, u32[]{:S(2)}) copy-start(f32[1,64,64]{2,1,0:T(8,128)} %fusion.3) | copy-start | bytes 49156

commit v3 on v2

--- a/solution.py
+++ b/solution.py
@@ -80,6 +80,17 @@
     return jnp.sum(chosen, axis=-1)
 
 
+def butterfly_sum(x, axes):
+    peers = 1
+    for axis in axes:
+        peers *= lax.axis_size(axis)
+    step = 1
+    while step < peers:
+        x = x + lax.ppermute(x, axes, [(i, i ^ step) for i in range(peers)])
+        step *= 2
+    return x
+
+
 def inner_products(left, right):
     return jnp.dot(
         left, right.T, precision=lax.Precision.HIGHEST, preferred_element_type=jnp.float32
@@ -128,7 +139,7 @@
             inner_products(flattened, image_flat) / total_rows,
         ]
     )
-    gram_matrix, raw_proj = jnp.sum(lax.all_gather(partial, ("row", "col")), axis=0)
+    gram_matrix, raw_proj = butterfly_sum(partial, ("row", "col"))
     upper_factor, inverse = factor_inverse(gram_matrix)
     orthonormal = jnp.dot(
         inverse, flattened, precision=lax.Precision.HIGHEST, preferred_element_type=jnp.float32

time: 73.2 us -> 64.8 us (0.89)
  blocking collectives: 25.2 us -> 0 us
  starting transfers between devices: 14.6 us -> 23.9 us
  waiting for transfers between devices: 8.45 us -> 16.9 us
    all_gather x1 -> x0, blocking collectives: 25.2 us -> none  [local(): lax.all_gather(partial, ('row', 'col'))]
    ppermute x0 -> x4, starting transfers between devices: none -> 9.31 us  [butterfly_sum(): x = x + lax.ppermute(x, axes, [(i, i ^ step) for i in range(peers)])]
    ppermute x0 -> x4, waiting for transfers between devices: none -> 7.14 us  [butterfly_sum(): x = x + lax.ppermute(x, axes, [(i, i ^ step) for i in range(peers)])]
    ppermute x2, waiting for transfers between devices: 0.73 us -> 1.58 us  [padded(): after = lax.ppermute(leading, axis, down)]
    unnamed x11 -> x8, local copies, waits for them, and re-layouts: 3.93 us -> 3.85 us
  transfers between devices with their start and end apart: 6 -> 10, of which waited for: 2 -> 6; matrix products, arithmetic and copies ran while one was open for 4% -> 4% of each run, Pallas kernels for 0% -> 0%
where the time goes in v3:
time: 64.8 us; the launch traced here: 64.5 us
  starting transfers between devices  23.9 us (37%)
  waiting for transfers between devices  16.9 us (26%)
  other arithmetic  13.5 us (21%)
  local copies, waits for them, and re-layouts  5.43 us (8%)
  matrix products  3.08 us (5%)
  between operations  1.63 us (3%)
    ppermute x4, starting transfers between devices, butterfly_sum(): x = x + lax.ppermute(x, axes, [(i, i ^ step) for i in range(peers)])  9.31 us
    ppermute x2, waiting for transfers between devices, padded(): before = lax.ppermute(last, axis, up)  8.2 us
    ppermute x4, waiting for transfers between devices, butterfly_sum(): x = x + lax.ppermute(x, axes, [(i, i ^ step) for i in range(peers)])  7.14 us
    another operation x3, other arithmetic, factor_inverse(): lower_factor = jnp.linalg.cholesky(gram_matrix)  6.52 us
    ppermute x2, starting transfers between devices, padded(): before = lax.ppermute(last, axis, up)  6.2 us
    ppermute x2, starting transfers between devices, shifted(): return lax.ppermute(x, axis, pairs)  5.84 us
    another operation x1, other arithmetic, factor_inverse(): lax.linalg.triangular_solve(lower_factor, jnp.eye(gram_matrix.shape[0], d...  4.9 us
    unnamed x8, local copies, waits for them, and re-layouts  3.85 us
  transfers between devices with their start and end apart: 10, of which 6 were waited for; matrix products, arithmetic and copies ran while one was open for 4% of the time, Pallas kernels for 0%

profile of v3, /device:TPU:0, one launch (start us, length us, event | category | flops | bytes accessed | tf_op | source)
XLA Modules:
  0.0 64.5 jit_solution(16472107353787378747)
XLA Ops:
  0.6 1.1 %copy.71 = f32[64,3,1,4,128]{4,0,3,2,1:T(8,128)S(1)} copy(f32[64,3,1,4,128]{4,3,2,1,0:T(4,128)} %param.5) | data formatting | bytes 786432 | tf_op args[0]
  1.7 4.9 %collective-permute-start.2 = (f32[64,3,1,4,128]{4,0,3,2,1:T(8,128)S(1)}, f32[64,3,1,4,128]{4,0,3,2,1:T(8,128)S(1)}, u32[]{:S(2)}, u32[]{:S(2)}) collective-permute-start(f32[64,3,1,4,128]{4,0,3,2,1:T(8,128)S(1)} %copy.71), channel_id=1, source_target_pairs={{0,2},{2,4},{4,6},{6,8},{8,10},{10,12},{12,14},{1,3},{3,5},{5,7},{... | collective-permute-start | bytes 1179656 | tf_op jit(solution)/shard_map/ppermute | solution.py:20
  6.6 1.3 %collective-permute-start.3 = (f32[64,3,1,4,128]{4,0,3,2,1:T(8,128)S(1)}, f32[64,3,1,4,128]{4,0,3,2,1:T(8,128)S(1)}, u32[]{:S(2)}, u32[]{:S(2)}) collective-permute-start(f32[64,3,1,4,128]{4,0,3,2,1:T(8,128)S(1)} %copy.71), channel_id=1, source_target_pairs={{2,0},{4,2},{6,4},{8,6},{10,8},{12,10},{14,12},{3,1},{5,3},{7,5},{... | collective-permute-start | bytes 1179656 | tf_op jit(solution)/shard_map/ppermute | solution.py:21
  7.9 0.8 %select_reduce_fusion.1 = (f32[4,128]{1,0:T(4,128)S(1)}, f32[4,128]{1,0:T(4,128)S(1)}) fusion(f32[8]{0:T(128)} %param.8, s32[4,128]{1,0:T(4,128)} %bitcast.88, f32[8]{0:T(128)} %param.7), kind=kLoop, calls=%fused_computation.54 | loop fusion | flops 19456 | bytes 6208 | tf_op jit(solution)/shard_map/reduce_sum | solution.py:80
  8.7 4.5 %collective-permute-start = (f32[1,4,128]{2,1,0:T(4,128)S(1)}, f32[1,4,128]{2,1,0:T(4,128)S(1)}, u32[]{:S(2)}, u32[]{:S(2)}) collective-permute-start(f32[1,4,128]{2,1,0:T(4,128)S(1)} %bitcast.85), channel_id=1, source_target_pairs={{0,2},{2,4},{4,6},{6,8},{8,10},{10,12},{12,14},{1,3},{3,5},{5,7},{... | collective-permute-start | bytes 6152 | tf_op jit(solution)/shard_map/ppermute | solution.py:10
  13.3 1.3 %collective-permute-start.1 = (f32[1,1,128]{2,1,0:T(1,128)S(1)}, f32[1,1,128]{2,1,0:T(1,128)S(1)}, u32[]{:S(2)}, u32[]{:S(2)}) collective-permute-start(f32[1,1,128]{2,1,0:T(1,128)S(1)} %slice.92), channel_id=1, source_target_pairs={{0,1},{2,3},{4,5},{6,7},{8,9},{10,11},{12,13},{14,15},{16,17},{18,... | collective-permute-start | bytes 1544 | tf_op jit(solution)/shard_map/ppermute | solution.py:10
  15.2 8.2 %collective-permute-done.2 = f32[64,3,1,4,128]{4,0,3,2,1:T(8,128)S(1)} collective-permute-done((f32[64,3,1,4,128]{4,0,3,2,1:T(8,128)S(1)}, f32[64,3,1,4,128]{4,0,3,2,1:T(8,128)S(1)}, u32[]{:S(2)}, u32[]{:S(2)}) %collective-permute-start.2) | collective-permute-done | bytes 393248 | tf_op jit(solution)/shard_map/ppermute | solution.py:20
  23.6 1.3 %collective-permute-start.4 = (f32[64,3,3,1,128]{4,0,3,2,1:T(8,128)S(1)}, f32[64,3,3,1,128]{4,0,3,2,1:T(8,128)S(1)}, u32[]{:S(2)}, u32[]{:S(2)}) collective-permute-start(f32[64,3,3,1,128]{4,0,3,2,1:T(8,128)S(1)} %get-tuple-element.25), channel_id=1, source_target_pairs={{0,1},{2,3},{4,5},{6,7},{8,9},{10,11},{12,13},{14,15},{16,17},{18,... | collective-permute-start | bytes 884744 | tf_op jit(solution)/shard_map/ppermute | solution.py:20
  24.9 1.3 %collective-permute-start.5 = (f32[64,3,3,1,128]{4,0,3,2,1:T(8,128)S(1)}, f32[64,3,3,1,128]{4,0,3,2,1:T(8,128)S(1)}, u32[]{:S(2)}, u32[]{:S(2)}) collective-permute-start(f32[64,3,3,1,128]{4,0,3,2,1:T(8,128)S(1)} %get-tuple-element.26), channel_id=1, source_target_pairs={{1,0},{3,2},{5,4},{7,6},{9,8},{11,10},{13,12},{15,14},{17,16},{19,... | collective-permute-start | bytes 884744 | tf_op jit(solution)/shard_map/ppermute | solution.py:21
  26.8 1.6 %collective-permute-done.5 = f32[64,3,3,1,128]{4,0,3,2,1:T(8,128)S(1)} collective-permute-done((f32[64,3,3,1,128]{4,0,3,2,1:T(8,128)S(1)}, f32[64,3,3,1,128]{4,0,3,2,1:T(8,128)S(1)}, u32[]{:S(2)}, u32[]{:S(2)}) %collective-permute-start.5) | collective-permute-done | bytes 294944 | tf_op jit(solution)/shard_map/ppermute | solution.py:21
  30.2 1.1 %collective-permute-done.6 = f32[2,64,64]{1,2,0:T(8,128)S(1)} collective-permute-done((f32[2,64,64]{1,2,0:T(8,128)S(1)}, f32[2,64,64]{1,2,0:T(8,128)S(1)}, u32[]{:S(2)}, u32[]{:S(2)}) %collective-permute-start.6) | collective-permute-done | bytes 32800 | tf_op jit(solution)/shard_map/ppermute | solution.py:89
  31.4 2.5 %collective-permute-start.7 = (f32[2,64,64]{1,2,0:T(8,128)S(1)}, f32[2,64,64]{1,2,0:T(8,128)S(1)}, u32[]{:S(2)}, u32[]{:S(2)}) collective-permute-start(f32[2,64,64]{1,2,0:T(8,128)S(1)} %fusion.28), channel_id=1, source_target_pairs={{0,2},{1,3},{2,0},{3,1},{4,6},{5,7},{6,4},{7,5},{8,10},{9,11},{10,... | collective-permute-start | bytes 98312 | tf_op jit(solution)/shard_map/ppermute | solution.py:89
  33.9 2.4 %collective-permute-done.7 = f32[2,64,64]{1,2,0:T(8,128)S(1)} collective-permute-done((f32[2,64,64]{1,2,0:T(8,128)S(1)}, f32[2,64,64]{1,2,0:T(8,128)S(1)}, u32[]{:S(2)}, u32[]{:S(2)}) %collective-permute-start.7) | collective-permute-done | bytes 32800 | tf_op jit(solution)/shard_map/ppermute | solution.py:89
  36.4 3.5 %collective-permute-start.8 = (f32[2,64,64]{1,2,0:T(8,128)S(1)}, f32[2,64,64]{1,2,0:T(8,128)S(1)}, u32[]{:S(2)}, u32[]{:S(2)}) collective-permute-start(f32[2,64,64]{1,2,0:T(8,128)S(1)} %fusion.34), channel_id=1, source_target_pairs={{0,4},{1,5},{2,6},{3,7},{4,0},{5,1},{6,2},{7,3},{8,12},{9,13},{10,... | collective-permute-start | bytes 98312 | tf_op jit(solution)/shard_map/ppermute | solution.py:89
  39.8 2.2 %collective-permute-done.8 = f32[2,64,64]{1,2,0:T(8,128)S(1)} collective-permute-done((f32[2,64,64]{1,2,0:T(8,128)S(1)}, f32[2,64,64]{1,2,0:T(8,128)S(1)}, u32[]{:S(2)}, u32[]{:S(2)}) %collective-permute-start.8) | collective-permute-done | bytes 32800 | tf_op jit(solution)/shard_map/ppermute | solution.py:89
  42.1 3.1 %collective-permute-start.9 = (f32[2,64,64]{1,2,0:T(8,128)S(1)}, f32[2,64,64]{1,2,0:T(8,128)S(1)}, u32[]{:S(2)}, u32[]{:S(2)}) collective-permute-start(f32[2,64,64]{1,2,0:T(8,128)S(1)} %add.35), channel_id=1, source_target_pairs={{0,8},{1,9},{2,10},{3,11},{4,12},{5,13},{6,14},{7,15},{8,0},{9,1},... | collective-permute-start | bytes 98312 | tf_op jit(solution)/shard_map/ppermute | solution.py:89
  46.1 1.4 %collective-permute-done.9 = f32[2,64,64]{1,2,0:T(8,128)S(1)} collective-permute-done((f32[2,64,64]{1,2,0:T(8,128)S(1)}, f32[2,64,64]{1,2,0:T(8,128)S(1)}, u32[]{:S(2)}, u32[]{:S(2)}) %collective-permute-start.9) | collective-permute-done | bytes 32800 | tf_op jit(solution)/shard_map/ppermute | solution.py:89
  47.5 5.8 %cholesky.17 = f32[64,64]{1,0:T(8,128)S(1)} custom-call(f32[64,64]{1,0:T(8,128)S(1)} %fusion.22), custom_call_target="Cholesky" | custom-call | tf_op jit(solution)/shard_map/jit(cholesky)/cholesky | solution.py:112
  54.1 0.7 %fusion.27 = (f32[64,64]{0,1:T(8,128)S(1)}, f32[1,64,64]{2,1,0:T(8,128)S(1)}) fusion(f32[64,64]{1,0:T(8,128)S(1)} %cholesky.17, pred[]{:T(512)} %compare_reduce_fusion), kind=kLoop, calls=%fused_computation.53 | loop fusion | flops 16384 | bytes 49153 | tf_op jit(solution)/shard_map/transpose | solution.py:116
  54.7 4.9 %custom-call.6 = f32[1,64,64]{1,2,0:T(8,128)S(1)} custom-call(f32[1,64,64]{2,1,0:T(8,128)S(1)} %get-tuple-element.34), custom_call_target="InvertDiagBlocksLowerTriangular" | custom-call | tf_op jit(solution)/shard_map/triangular_solve | solution.py:113
  60.1 0.8 %fusion.30 = f32[64,64]{1,0:T(8,128)} fusion(f32[64,64]{1,0:T(8,128)S(1)} %fusion.21, f32[64,64]{1,0:T(8,128)S(1)} %fusion.25), kind=kOutput, calls=%fused_computation.66 | convolution fusion | flops 3145728 | bytes 49152 | tf_op jit(solution)/shard_map/dot_general | solution.py:95
  61.3 1.0 %copy.83 = f32[64,3,1,4,128]{4,3,2,1,0:T(4,128)} copy(f32[64,3,1,4,128]{4,0,3,1,2:T(8,128)S(1)} %convolution_bitcast_fusion) | data formatting | bytes 786432
  62.8 1.0 %copy.81 = f32[64,3,1,4,128]{4,3,2,1,0:T(4,128)} copy(f32[64,3,1,4,128]{4,0,3,1,2:T(8,128)S(1)} %convolution_bitcast_fusion.1) | data formatting | bytes 786432
  63.8 0.7 %copy.82 = f32[64,64]{1,0:T(8,128)} copy(f32[64,64]{0,1:T(8,128)S(1)} %get-tuple-element.33) | data formatting | bytes 32768
  (45 shorter events, 5.5 us)
Async XLA Ops:
  0.6 22.8 %copy-start = (f32[64,3,1,4,128]{4,3,2,1,0:T(4,128)S(1)}, f32[64,3,1,4,128]{4,3,2,1,0:T(4,128)}, u32[]{:S(2)}) copy-start(f32[64,3,1,4,128]{4,3,2,1,0:T(4,128)} %param.5) | copy-start | bytes 1179652
  1.7 21.7 %collective-permute-start.2 = (f32[64,3,1,4,128]{4,0,3,2,1:T(8,128)S(1)}, f32[64,3,1,4,128]{4,0,3,2,1:T(8,128)S(1)}, u32[]{:S(2)}, u32[]{:S(2)}) collective-permute-start(f32[64,3,1,4,128]{4,0,3,2,1:T(8,128)S(1)} %copy.71), channel_id=1, source_target_pairs={{0,2},{2,4},{4,6},{6,8},{8,10},{10,12},{12,14},{1,3},{3,5},{5,7},{... | collective-permute-start | bytes 1179656 | tf_op jit(solution)/shard_map/ppermute | solution.py:20
  6.6 16.9 %collective-permute-start.3 = (f32[64,3,1,4,128]{4,0,3,2,1:T(8,128)S(1)}, f32[64,3,1,4,128]{4,0,3,2,1:T(8,128)S(1)}, u32[]{:S(2)}, u32[]{:S(2)}) collective-permute-start(f32[64,3,1,4,128]{4,0,3,2,1:T(8,128)S(1)} %copy.71), channel_id=1, source_target_pairs={{2,0},{4,2},{6,4},{8,6},{10,8},{12,10},{14,12},{3,1},{5,3},{7,5},{... | collective-permute-start | bytes 1179656 | tf_op jit(solution)/shard_map/ppermute | solution.py:21
  8.7 18.1 %collective-permute-start = (f32[1,4,128]{2,1,0:T(4,128)S(1)}, f32[1,4,128]{2,1,0:T(4,128)S(1)}, u32[]{:S(2)}, u32[]{:S(2)}) collective-permute-start(f32[1,4,128]{2,1,0:T(4,128)S(1)} %bitcast.85), channel_id=1, source_target_pairs={{0,2},{2,4},{4,6},{6,8},{8,10},{10,12},{12,14},{1,3},{3,5},{5,7},{... | collective-permute-start | bytes 6152 | tf_op jit(solution)/shard_map/ppermute | solution.py:10
  13.3 13.5 %collective-permute-start.1 = (f32[1,1,128]{2,1,0:T(1,128)S(1)}, f32[1,1,128]{2,1,0:T(1,128)S(1)}, u32[]{:S(2)}, u32[]{:S(2)}) collective-permute-start(f32[1,1,128]{2,1,0:T(1,128)S(1)} %slice.92), channel_id=1, source_target_pairs={{0,1},{2,3},{4,5},{6,7},{8,9},{10,11},{12,13},{14,15},{16,17},{18,... | collective-permute-start | bytes 1544 | tf_op jit(solution)/shard_map/ppermute | solution.py:10
  23.6 3.2 %collective-permute-start.4 = (f32[64,3,3,1,128]{4,0,3,2,1:T(8,128)S(1)}, f32[64,3,3,1,128]{4,0,3,2,1:T(8,128)S(1)}, u32[]{:S(2)}, u32[]{:S(2)}) collective-permute-start(f32[64,3,3,1,128]{4,0,3,2,1:T(8,128)S(1)} %get-tuple-element.25), channel_id=1, source_target_pairs={{0,1},{2,3},{4,5},{6,7},{8,9},{10,11},{12,13},{14,15},{16,17},{18,... | collective-permute-start | bytes 884744 | tf_op jit(solution)/shard_map/ppermute | solution.py:20
  24.9 3.5 %collective-permute-start.5 = (f32[64,3,3,1,128]{4,0,3,2,1:T(8,128)S(1)}, f32[64,3,3,1,128]{4,0,3,2,1:T(8,128)S(1)}, u32[]{:S(2)}, u32[]{:S(2)}) collective-permute-start(f32[64,3,3,1,128]{4,0,3,2,1:T(8,128)S(1)} %get-tuple-element.26), channel_id=1, source_target_pairs={{1,0},{3,2},{5,4},{7,6},{9,8},{11,10},{13,12},{15,14},{17,16},{19,... | collective-permute-start | bytes 884744 | tf_op jit(solution)/shard_map/ppermute | solution.py:21
  30.0 1.3 %collective-permute-start.6 = (f32[2,64,64]{1,2,0:T(8,128)S(1)}, f32[2,64,64]{1,2,0:T(8,128)S(1)}, u32[]{:S(2)}, u32[]{:S(2)}) collective-permute-start(f32[2,64,64]{1,2,0:T(8,128)S(1)} %pad_maximum_fusion.1), channel_id=1, source_target_pairs={{0,1},{1,0},{2,3},{3,2},{4,5},{5,4},{6,7},{7,6},{8,9},{9,8},{10,11... | collective-permute-start | bytes 98312 | tf_op jit(solution)/shard_map/ppermute | solution.py:89
  31.4 5.0 %collective-permute-start.7 = (f32[2,64,64]{1,2,0:T(8,128)S(1)}, f32[2,64,64]{1,2,0:T(8,128)S(1)}, u32[]{:S(2)}, u32[]{:S(2)}) collective-permute-start(f32[2,64,64]{1,2,0:T(8,128)S(1)} %fusion.28), channel_id=1, source_target_pairs={{0,2},{1,3},{2,0},{3,1},{4,6},{5,7},{6,4},{7,5},{8,10},{9,11},{10,... | collective-permute-start | bytes 98312 | tf_op jit(solution)/shard_map/ppermute | solution.py:89
  36.4 5.7 %collective-permute-start.8 = (f32[2,64,64]{1,2,0:T(8,128)S(1)}, f32[2,64,64]{1,2,0:T(8,128)S(1)}, u32[]{:S(2)}, u32[]{:S(2)}) collective-permute-start(f32[2,64,64]{1,2,0:T(8,128)S(1)} %fusion.34), channel_id=1, source_target_pairs={{0,4},{1,5},{2,6},{3,7},{4,0},{5,1},{6,2},{7,3},{8,12},{9,13},{10,... | collective-permute-start | bytes 98312 | tf_op jit(solution)/shard_map/ppermute | solution.py:89
  42.1 5.3 %collective-permute-start.9 = (f32[2,64,64]{1,2,0:T(8,128)S(1)}, f32[2,64,64]{1,2,0:T(8,128)S(1)}, u32[]{:S(2)}, u32[]{:S(2)}) collective-permute-start(f32[2,64,64]{1,2,0:T(8,128)S(1)} %add.35), channel_id=1, source_target_pairs={{0,8},{1,9},{2,10},{3,11},{4,12},{5,13},{6,14},{7,15},{8,0},{9,1},... | collective-permute-start | bytes 98312 | tf_op jit(solution)/shard_map/ppermute | solution.py:89

commit v4 on v3

--- a/solution.py
+++ b/solution.py
@@ -121,6 +121,7 @@
     flattened = krylov_basis.reshape(columns, -1)
     total_rows = flattened.shape[1] * lax.axis_size("row") * lax.axis_size("col")
     cells_y = regions.shape[1]
+    gram_matrix = butterfly_sum(inner_products(flattened, flattened) / total_rows, ("row", "col"))
     local_mu = lookup(regions, mu_table)
     from_lower_row = shifted(local_mu, "row", 1)
     from_lower_col = shifted(local_mu[:, cells_y - 1 :], "col", 1)
@@ -133,13 +134,7 @@
     padded_basis = padded(krylov_basis, (("row", 2), ("col", 3)), 1)
     image_basis = operator_block(padded_basis, coupling, permittivity, shift_scalar)
     image_flat = image_basis.reshape(columns, -1)
-    partial = jnp.stack(
-        [
-            inner_products(flattened, flattened) / total_rows,
-            inner_products(flattened, image_flat) / total_rows,
-        ]
-    )
-    gram_matrix, raw_proj = butterfly_sum(partial, ("row", "col"))
+    raw_proj = butterfly_sum(inner_products(flattened, image_flat) / total_rows, ("row", "col"))
     upper_factor, inverse = factor_inverse(gram_matrix)
     orthonormal = jnp.dot(
         inverse, flattened, precision=lax.Precision.HIGHEST, preferred_element_type=jnp.float32

time: 64.8 us -> 69.5 us (1.073)
  starting transfers between devices: 23.9 us -> 28.6 us
  matrix products: 3.08 us -> 4.2 us
  other arithmetic: 13.5 us -> 12.8 us
    ppermute x4 -> x8, waiting for transfers between devices: 7.14 us -> 16.6 us  [butterfly_sum(): x = x + lax.ppermute(x, axes, [(i, i ^ step) for i in range(peers)])]
    ppermute x2, waiting for transfers between devices: 8.2 us -> 0.01 us  [padded(): before = lax.ppermute(last, axis, up)]
    ppermute x4 -> x8, starting transfers between devices: 9.31 us -> 16.8 us  [butterfly_sum(): x = x + lax.ppermute(x, axes, [(i, i ^ step) for i in range(peers)])]
    ppermute x2, starting transfers between devices: 5.84 us -> 3.5 us  [shifted(): return lax.ppermute(x, axis, pairs)]
    ppermute x2, waiting for transfers between devices: 1.58 us -> 0.01 us  [padded(): after = lax.ppermute(leading, axis, down)]
    dot_general x3, matrix products: 1.73 us -> 2.89 us  [inner_products(): jnp.dot(left, right.T, precision=lax.Precision.HIGHEST, preferred_element...]
    unnamed x8 -> x14, local copies, waits for them, and re-layouts: 3.85 us -> 3.8 us
  transfers between devices with their start and end apart: 10 -> 14, of which waited for: 6 -> 5; matrix products, arithmetic and copies ran while one was open for 4% -> 26% of each run, Pallas kernels for 0% -> 0%
where the time goes in v4:
time: 69.5 us; the launch traced here: 69.2 us
  starting transfers between devices  28.6 us (41%)
  waiting for transfers between devices  16.6 us (24%)
  other arithmetic  12.8 us (18%)
  local copies, waits for them, and re-layouts  5.3 us (8%)
  matrix products  4.2 us (6%)
  between operations  1.65 us (2%)
    ppermute x8, starting transfers between devices, butterfly_sum(): x = x + lax.ppermute(x, axes, [(i, i ^ step) for i in range(peers)])  16.8 us
    ppermute x8, waiting for transfers between devices, butterfly_sum(): x = x + lax.ppermute(x, axes, [(i, i ^ step) for i in range(peers)])  16.6 us
    another operation x3, other arithmetic, factor_inverse(): lower_factor = jnp.linalg.cholesky(gram_matrix)  6.52 us
    ppermute x2, starting transfers between devices, padded(): before = lax.ppermute(last, axis, up)  5.73 us
    another operation x1, other arithmetic, factor_inverse(): lax.linalg.triangular_solve(lower_factor, jnp.eye(gram_matrix.shape[0], d...  4.9 us
    unnamed x14, local copies, waits for them, and re-layouts  3.8 us
    ppermute x2, starting transfers between devices, shifted(): return lax.ppermute(x, axis, pairs)  3.5 us
    dot_general x3, matrix products, inner_products(): jnp.dot(left, right.T, precision=lax.Precision.HIGHEST, preferred_element...  2.89 us
  transfers between devices with their start and end apart: 14, of which 5 were waited for; matrix products, arithmetic and copies ran while one was open for 26% of the time, Pallas kernels for 0%

profile of v4, /device:TPU:0, one launch (start us, length us, event | category | flops | bytes accessed | tf_op | source)
XLA Modules:
  0.0 69.2 jit_solution(10839584071676281910)
XLA Ops:
  0.7 1.6 %fusion.2 = f32[64,64]{0,1:T(8,128)S(1)} fusion(f32[64,3,4,128]{3,2,1,0:T(4,128)} %bitcast.65), kind=kOutput, calls=%fused_computation.7 | convolution fusion | flops 75501568 | bytes 409600 | tf_op jit(solution)/shard_map/dot_general | solution.py:95
  2.9 1.0 %copy.77 = f32[64,3,1,4,128]{4,0,3,2,1:T(8,128)S(1)} copy(f32[64,3,1,4,128]{4,3,2,1,0:T(4,128)} %param.5) | data formatting | bytes 786432 | tf_op args[0]
  3.9 4.4 %collective-permute-start.6 = (f32[64,3,1,4,128]{4,0,3,2,1:T(8,128)S(1)}, f32[64,3,1,4,128]{4,0,3,2,1:T(8,128)S(1)}, u32[]{:S(2)}, u32[]{:S(2)}) collective-permute-start(f32[64,3,1,4,128]{4,0,3,2,1:T(8,128)S(1)} %copy.77), channel_id=1, source_target_pairs={{0,2},{2,4},{4,6},{6,8},{8,10},{10,12},{12,14},{1,3},{3,5},{5,7},{... | collective-permute-start | bytes 1179656 | tf_op jit(solution)/shard_map/ppermute | solution.py:20
  8.3 1.3 %collective-permute-start.7 = (f32[64,3,1,4,128]{4,0,3,2,1:T(8,128)S(1)}, f32[64,3,1,4,128]{4,0,3,2,1:T(8,128)S(1)}, u32[]{:S(2)}, u32[]{:S(2)}) collective-permute-start(f32[64,3,1,4,128]{4,0,3,2,1:T(8,128)S(1)} %copy.77), channel_id=1, source_target_pairs={{2,0},{4,2},{6,4},{8,6},{10,8},{12,10},{14,12},{3,1},{5,3},{7,5},{... | collective-permute-start | bytes 1179656 | tf_op jit(solution)/shard_map/ppermute | solution.py:21
  9.6 2.7 %collective-permute-start.1 = (f32[64,64]{0,1:T(8,128)S(1)}, f32[64,64]{0,1:T(8,128)S(1)}, u32[]{:S(2)}, u32[]{:S(2)}) collective-permute-start(f32[64,64]{0,1:T(8,128)S(1)} %add.45), channel_id=1, source_target_pairs={{0,2},{1,3},{2,0},{3,1},{4,6},{5,7},{6,4},{7,5},{8,10},{9,11},{10,... | collective-permute-start | bytes 49160 | tf_op jit(solution)/shard_map/ppermute | solution.py:89
  12.4 1.9 %collective-permute-start.4 = (f32[1,4,128]{2,1,0:T(4,128)S(1)}, f32[1,4,128]{2,1,0:T(4,128)S(1)}, u32[]{:S(2)}, u32[]{:S(2)}) collective-permute-start(f32[1,4,128]{2,1,0:T(4,128)S(1)} %bitcast.69), channel_id=1, source_target_pairs={{0,2},{2,4},{4,6},{6,8},{8,10},{10,12},{12,14},{1,3},{3,5},{5,7},{... | collective-permute-start | bytes 6152 | tf_op jit(solution)/shard_map/ppermute | solution.py:10
  14.4 1.6 %collective-permute-start.5 = (f32[1,1,128]{2,1,0:T(1,128)S(1)}, f32[1,1,128]{2,1,0:T(1,128)S(1)}, u32[]{:S(2)}, u32[]{:S(2)}) collective-permute-start(f32[1,1,128]{2,1,0:T(1,128)S(1)} %slice.92), channel_id=1, source_target_pairs={{0,1},{2,3},{4,5},{6,7},{8,9},{10,11},{12,13},{14,15},{16,17},{18,... | collective-permute-start | bytes 1544 | tf_op jit(solution)/shard_map/ppermute | solution.py:10
  16.6 9.8 %collective-permute-done.1 = f32[64,64]{0,1:T(8,128)S(1)} collective-permute-done((f32[64,64]{0,1:T(8,128)S(1)}, f32[64,64]{0,1:T(8,128)S(1)}, u32[]{:S(2)}, u32[]{:S(2)}) %collective-permute-start.1) | collective-permute-done | bytes 16416 | tf_op jit(solution)/shard_map/ppermute | solution.py:89
  26.5 3.5 %collective-permute-start.2 = (f32[64,64]{0,1:T(8,128)S(1)}, f32[64,64]{0,1:T(8,128)S(1)}, u32[]{:S(2)}, u32[]{:S(2)}) collective-permute-start(f32[64,64]{0,1:T(8,128)S(1)} %add.46), channel_id=1, source_target_pairs={{0,4},{1,5},{2,6},{3,7},{4,0},{5,1},{6,2},{7,3},{8,12},{9,13},{10,... | collective-permute-start | bytes 49160 | tf_op jit(solution)/shard_map/ppermute | solution.py:89
  30.3 1.6 %collective-permute-done.2 = f32[64,64]{0,1:T(8,128)S(1)} collective-permute-done((f32[64,64]{0,1:T(8,128)S(1)}, f32[64,64]{0,1:T(8,128)S(1)}, u32[]{:S(2)}, u32[]{:S(2)}) %collective-permute-start.2) | collective-permute-done | bytes 16416 | tf_op jit(solution)/shard_map/ppermute | solution.py:89
  31.8 3.0 %collective-permute-start.3 = (f32[64,64]{0,1:T(8,128)S(1)}, f32[64,64]{0,1:T(8,128)S(1)}, u32[]{:S(2)}, u32[]{:S(2)}) collective-permute-start(f32[64,64]{0,1:T(8,128)S(1)} %add.47), channel_id=1, source_target_pairs={{0,8},{1,9},{2,10},{3,11},{4,12},{5,13},{6,14},{7,15},{8,0},{9,1},... | collective-permute-start | bytes 49160 | tf_op jit(solution)/shard_map/ppermute | solution.py:89
  34.9 1.9 %collective-permute-done.3 = f32[64,64]{0,1:T(8,128)S(1)} collective-permute-done((f32[64,64]{0,1:T(8,128)S(1)}, f32[64,64]{0,1:T(8,128)S(1)}, u32[]{:S(2)}, u32[]{:S(2)}) %collective-permute-start.3) | collective-permute-done | bytes 16416 | tf_op jit(solution)/shard_map/ppermute | solution.py:89
  37.0 1.3 %collective-permute-start.8 = (f32[64,3,3,1,128]{4,0,3,2,1:T(8,128)S(1)}, f32[64,3,3,1,128]{4,0,3,2,1:T(8,128)S(1)}, u32[]{:S(2)}, u32[]{:S(2)}) collective-permute-start(f32[64,3,3,1,128]{4,0,3,2,1:T(8,128)S(1)} %get-tuple-element.25), channel_id=1, source_target_pairs={{0,1},{2,3},{4,5},{6,7},{8,9},{10,11},{12,13},{14,15},{16,17},{18,... | collective-permute-start | bytes 884744 | tf_op jit(solution)/shard_map/ppermute | solution.py:20
  38.4 1.3 %collective-permute-start.9 = (f32[64,3,3,1,128]{4,0,3,2,1:T(8,128)S(1)}, f32[64,3,3,1,128]{4,0,3,2,1:T(8,128)S(1)}, u32[]{:S(2)}, u32[]{:S(2)}) collective-permute-start(f32[64,3,3,1,128]{4,0,3,2,1:T(8,128)S(1)} %get-tuple-element.26), channel_id=1, source_target_pairs={{1,0},{3,2},{5,4},{7,6},{9,8},{11,10},{13,12},{15,14},{17,16},{19,... | collective-permute-start | bytes 884744 | tf_op jit(solution)/shard_map/ppermute | solution.py:21
  39.7 5.8 %cholesky.17 = f32[64,64]{1,0:T(8,128)S(1)} custom-call(f32[64,64]{1,0:T(8,128)S(1)} %fusion.24), custom_call_target="Cholesky" | custom-call | tf_op jit(solution)/shard_map/jit(cholesky)/cholesky | solution.py:112
  47.8 1.2 %collective-permute-start.10 = (f32[64,64]{1,0:T(8,128)S(1)}, f32[64,64]{1,0:T(8,128)S(1)}, u32[]{:S(2)}, u32[]{:S(2)}) collective-permute-start(f32[64,64]{1,0:T(8,128)S(1)} %fusion.1), channel_id=1, source_target_pairs={{0,1},{1,0},{2,3},{3,2},{4,5},{5,4},{6,7},{7,6},{8,9},{9,8},{10,11... | collective-permute-start | bytes 49160 | tf_op jit(solution)/shard_map/ppermute | solution.py:89
  49.7 4.9 %custom-call.6 = f32[1,64,64]{1,2,0:T(8,128)S(1)} custom-call(f32[1,64,64]{2,1,0:T(8,128)S(1)} %get-tuple-element.34), custom_call_target="InvertDiagBlocksLowerTriangular" | custom-call | tf_op jit(solution)/shard_map/triangular_solve | solution.py:113
  54.6 1.0 %collective-permute-start.11 = (f32[64,64]{1,0:T(8,128)S(1)}, f32[64,64]{1,0:T(8,128)S(1)}, u32[]{:S(2)}, u32[]{:S(2)}) collective-permute-start(f32[64,64]{1,0:T(8,128)S(1)} %add.50), channel_id=1, source_target_pairs={{0,2},{1,3},{2,0},{3,1},{4,6},{5,7},{6,4},{7,5},{8,10},{9,11},{10,... | collective-permute-start | bytes 49160 | tf_op jit(solution)/shard_map/ppermute | solution.py:89
  55.8 2.8 %collective-permute-done.11 = f32[64,64]{1,0:T(8,128)S(1)} collective-permute-done((f32[64,64]{1,0:T(8,128)S(1)}, f32[64,64]{1,0:T(8,128)S(1)}, u32[]{:S(2)}, u32[]{:S(2)}) %collective-permute-start.11) | collective-permute-done | bytes 16416 | tf_op jit(solution)/shard_map/ppermute | solution.py:89
  58.6 1.9 %collective-permute-start.12 = (f32[64,64]{1,0:T(8,128)S(1)}, f32[64,64]{1,0:T(8,128)S(1)}, u32[]{:S(2)}, u32[]{:S(2)}) collective-permute-start(f32[64,64]{1,0:T(8,128)S(1)} %add.51), channel_id=1, source_target_pairs={{0,4},{1,5},{2,6},{3,7},{4,0},{5,1},{6,2},{7,3},{8,12},{9,13},{10,... | collective-permute-start | bytes 49160 | tf_op jit(solution)/shard_map/ppermute | solution.py:89
  61.0 1.0 %copy.85 = f32[64,3,1,4,128]{4,3,2,1,0:T(4,128)} copy(f32[64,3,1,4,128]{4,0,3,1,2:T(8,128)S(1)} %convolution_bitcast_fusion.1) | data formatting | bytes 786432
  63.3 2.9 %collective-permute-start.13 = (f32[64,64]{1,0:T(8,128)S(1)}, f32[64,64]{1,0:T(8,128)S(1)}, u32[]{:S(2)}, u32[]{:S(2)}) collective-permute-start(f32[64,64]{1,0:T(8,128)S(1)} %add.52), channel_id=1, source_target_pairs={{0,8},{1,9},{2,10},{3,11},{4,12},{5,13},{6,14},{7,15},{8,0},{9,1},... | collective-permute-start | bytes 49160 | tf_op jit(solution)/shard_map/ppermute | solution.py:89
  66.7 1.0 %copy.87 = f32[64,3,1,4,128]{4,3,2,1,0:T(4,128)} copy(f32[64,3,1,4,128]{4,0,3,1,2:T(8,128)S(1)} %convolution_bitcast_fusion) | data formatting | bytes 786432
  68.4 0.8 %fusion.29 = f32[64,64]{1,0:T(8,128)} fusion(f32[64,64]{1,0:T(8,128)S(1)} %fusion.25, f32[64,64]{1,0:T(8,128)S(1)} %fusion.22), kind=kOutput, calls=%fused_computation.62 | convolution fusion | flops 3145728 | bytes 49152 | tf_op jit(solution)/shard_map/dot_general | solution.py:95
  (59 shorter events, 7.2 us)
Async XLA Ops:
  0.6 29.3 %copy-start = (f32[64,3,1,4,128]{4,3,2,1,0:T(4,128)S(1)}, f32[64,3,1,4,128]{4,3,2,1,0:T(4,128)}, u32[]{:S(2)}) copy-start(f32[64,3,1,4,128]{4,3,2,1,0:T(4,128)} %param.5) | copy-start | bytes 1179652
  0.6 11.7 %copy-start.1 = (s32[1,4,128]{2,1,0:T(4,128)S(1)}, s32[1,4,128]{2,1,0:T(4,128)}, u32[]{:S(2)}) copy-start(s32[1,4,128]{2,1,0:T(4,128)} %param.6) | copy-start | bytes 6148
  0.7 11.7 %copy-start.3 = (f32[8]{0:T(128)S(1)}, f32[8]{0:T(128)}, u32[]{:S(2)}) copy-start(f32[8]{0:T(128)} %param.7) | copy-start | bytes 100
  0.7 11.7 %copy-start.2 = (f32[8]{0:T(128)S(1)}, f32[8]{0:T(128)}, u32[]{:S(2)}) copy-start(f32[8]{0:T(128)} %param.8) | copy-start | bytes 100
  2.3 7.3 %collective-permute-start = (f32[64,64]{0,1:T(8,128)S(1)}, f32[64,64]{0,1:T(8,128)S(1)}, u32[]{:S(2)}, u32[]{:S(2)}) collective-permute-start(f32[64,64]{0,1:T(8,128)S(1)} %fusion.2), channel_id=1, source_target_pairs={{0,1},{1,0},{2,3},{3,2},{4,5},{5,4},{6,7},{7,6},{8,9},{9,8},{10,11... | collective-permute-start | bytes 49160 | tf_op jit(solution)/shard_map/ppermute | solution.py:89
  3.9 33.0 %collective-permute-start.6 = (f32[64,3,1,4,128]{4,0,3,2,1:T(8,128)S(1)}, f32[64,3,1,4,128]{4,0,3,2,1:T(8,128)S(1)}, u32[]{:S(2)}, u32[]{:S(2)}) collective-permute-start(f32[64,3,1,4,128]{4,0,3,2,1:T(8,128)S(1)} %copy.77), channel_id=1, source_target_pairs={{0,2},{2,4},{4,6},{6,8},{8,10},{10,12},{12,14},{1,3},{3,5},{5,7},{... | collective-permute-start | bytes 1179656 | tf_op jit(solution)/shard_map/ppermute | solution.py:20
  8.3 28.6 %collective-permute-start.7 = (f32[64,3,1,4,128]{4,0,3,2,1:T(8,128)S(1)}, f32[64,3,1,4,128]{4,0,3,2,1:T(8,128)S(1)}, u32[]{:S(2)}, u32[]{:S(2)}) collective-permute-start(f32[64,3,1,4,128]{4,0,3,2,1:T(8,128)S(1)} %copy.77), channel_id=1, source_target_pairs={{2,0},{4,2},{6,4},{8,6},{10,8},{12,10},{14,12},{3,1},{5,3},{7,5},{... | collective-permute-start | bytes 1179656 | tf_op jit(solution)/shard_map/ppermute | solution.py:21
  9.6 16.8 %collective-permute-start.1 = (f32[64,64]{0,1:T(8,128)S(1)}, f32[64,64]{0,1:T(8,128)S(1)}, u32[]{:S(2)}, u32[]{:S(2)}) collective-permute-start(f32[64,64]{0,1:T(8,128)S(1)} %add.45), channel_id=1, source_target_pairs={{0,2},{1,3},{2,0},{3,1},{4,6},{5,7},{6,4},{7,5},{8,10},{9,11},{10,... | collective-permute-start | bytes 49160 | tf_op jit(solution)/shard_map/ppermute | solution.py:89
  12.4 22.4 %collective-permute-start.4 = (f32[1,4,128]{2,1,0:T(4,128)S(1)}, f32[1,4,128]{2,1,0:T(4,128)S(1)}, u32[]{:S(2)}, u32[]{:S(2)}) collective-permute-start(f32[1,4,128]{2,1,0:T(4,128)S(1)} %bitcast.69), channel_id=1, source_target_pairs={{0,2},{2,4},{4,6},{6,8},{8,10},{10,12},{12,14},{1,3},{3,5},{5,7},{... | collective-permute-start | bytes 6152 | tf_op jit(solution)/shard_map/ppermute | solution.py:10
  14.4 20.5 %collective-permute-start.5 = (f32[1,1,128]{2,1,0:T(1,128)S(1)}, f32[1,1,128]{2,1,0:T(1,128)S(1)}, u32[]{:S(2)}, u32[]{:S(2)}) collective-permute-start(f32[1,1,128]{2,1,0:T(1,128)S(1)} %slice.92), channel_id=1, source_target_pairs={{0,1},{2,3},{4,5},{6,7},{8,9},{10,11},{12,13},{14,15},{16,17},{18,... | collective-permute-start | bytes 1544 | tf_op jit(solution)/shard_map/ppermute | solution.py:10
  26.5 5.4 %collective-permute-start.2 = (f32[64,64]{0,1:T(8,128)S(1)}, f32[64,64]{0,1:T(8,128)S(1)}, u32[]{:S(2)}, u32[]{:S(2)}) collective-permute-start(f32[64,64]{0,1:T(8,128)S(1)} %add.46), channel_id=1, source_target_pairs={{0,4},{1,5},{2,6},{3,7},{4,0},{5,1},{6,2},{7,3},{8,12},{9,13},{10,... | collective-permute-start | bytes 49160 | tf_op jit(solution)/shard_map/ppermute | solution.py:89
  31.8 4.9 %collective-permute-start.3 = (f32[64,64]{0,1:T(8,128)S(1)}, f32[64,64]{0,1:T(8,128)S(1)}, u32[]{:S(2)}, u32[]{:S(2)}) collective-permute-start(f32[64,64]{0,1:T(8,128)S(1)} %add.47), channel_id=1, source_target_pairs={{0,8},{1,9},{2,10},{3,11},{4,12},{5,13},{6,14},{7,15},{8,0},{9,1},... | collective-permute-start | bytes 49160 | tf_op jit(solution)/shard_map/ppermute | solution.py:89
  37.0 9.2 %collective-permute-start.8 = (f32[64,3,3,1,128]{4,0,3,2,1:T(8,128)S(1)}, f32[64,3,3,1,128]{4,0,3,2,1:T(8,128)S(1)}, u32[]{:S(2)}, u32[]{:S(2)}) collective-permute-start(f32[64,3,3,1,128]{4,0,3,2,1:T(8,128)S(1)} %get-tuple-element.25), channel_id=1, source_target_pairs={{0,1},{2,3},{4,5},{6,7},{8,9},{10,11},{12,13},{14,15},{16,17},{18,... | collective-permute-start | bytes 884744 | tf_op jit(solution)/shard_map/ppermute | solution.py:20
  38.4 7.8 %collective-permute-start.9 = (f32[64,3,3,1,128]{4,0,3,2,1:T(8,128)S(1)}, f32[64,3,3,1,128]{4,0,3,2,1:T(8,128)S(1)}, u32[]{:S(2)}, u32[]{:S(2)}) collective-permute-start(f32[64,3,3,1,128]{4,0,3,2,1:T(8,128)S(1)} %get-tuple-element.26), channel_id=1, source_target_pairs={{1,0},{3,2},{5,4},{7,6},{9,8},{11,10},{13,12},{15,14},{17,16},{19,... | collective-permute-start | bytes 884744 | tf_op jit(solution)/shard_map/ppermute | solution.py:21
  47.8 6.8 %collective-permute-start.10 = (f32[64,64]{1,0:T(8,128)S(1)}, f32[64,64]{1,0:T(8,128)S(1)}, u32[]{:S(2)}, u32[]{:S(2)}) collective-permute-start(f32[64,64]{1,0:T(8,128)S(1)} %fusion.1), channel_id=1, source_target_pairs={{0,1},{1,0},{2,3},{3,2},{4,5},{5,4},{6,7},{7,6},{8,9},{9,8},{10,11... | collective-permute-start | bytes 49160 | tf_op jit(solution)/shard_map/ppermute | solution.py:89
  54.6 4.0 %collective-permute-start.11 = (f32[64,64]{1,0:T(8,128)S(1)}, f32[64,64]{1,0:T(8,128)S(1)}, u32[]{:S(2)}, u32[]{:S(2)}) collective-permute-start(f32[64,64]{1,0:T(8,128)S(1)} %add.50), channel_id=1, source_target_pairs={{0,2},{1,3},{2,0},{3,1},{4,6},{5,7},{6,4},{7,5},{8,10},{9,11},{10,... | collective-permute-start | bytes 49160 | tf_op jit(solution)/shard_map/ppermute | solution.py:89
  58.6 4.7 %collective-permute-start.12 = (f32[64,64]{1,0:T(8,128)S(1)}, f32[64,64]{1,0:T(8,128)S(1)}, u32[]{:S(2)}, u32[]{:S(2)}) collective-permute-start(f32[64,64]{1,0:T(8,128)S(1)} %add.51), channel_id=1, source_target_pairs={{0,4},{1,5},{2,6},{3,7},{4,0},{5,1},{6,2},{7,3},{8,12},{9,13},{10,... | collective-permute-start | bytes 49160 | tf_op jit(solution)/shard_map/ppermute | solution.py:89
  63.3 4.9 %collective-permute-start.13 = (f32[64,64]{1,0:T(8,128)S(1)}, f32[64,64]{1,0:T(8,128)S(1)}, u32[]{:S(2)}, u32[]{:S(2)}) collective-permute-start(f32[64,64]{1,0:T(8,128)S(1)} %add.52), channel_id=1, source_target_pairs={{0,8},{1,9},{2,10},{3,11},{4,12},{5,13},{6,14},{7,15},{8,0},{9,1},... | collective-permute-start | bytes 49160 | tf_op jit(solution)/shard_map/ppermute | solution.py:89

commit v5 on v3

--- a/solution.py
+++ b/solution.py
@@ -11,14 +11,18 @@
 
 
 def padded(x, sides, width):
-    for axis, dim in sides:
+    for axis, dim, unused in sides:
         peers, length = (lax.axis_size(axis), x.shape[dim])
         up = [(i, (i + 1) % peers) for i in range(peers - 1)]
         down = [(j, i) for i, j in up]
         last = lax.slice_in_dim(x, length - width, length, axis=dim)
         leading = lax.slice_in_dim(x, 0, width, axis=dim)
+        kept = [c for c in range(x.shape[1]) if c != unused]
         before = lax.ppermute(last, axis, up)
-        after = lax.ppermute(leading, axis, down)
+        sent = lax.ppermute(jnp.concatenate([leading[:, c : c + 1] for c in kept], axis=1), axis, down)
+        parts = [sent[:, i : i + 1] for i in range(len(kept))]
+        parts.insert(unused, jnp.zeros_like(parts[0]))
+        after = jnp.concatenate(parts, axis=1)
         x = jnp.concatenate([before, x, after], axis=dim)
     return x
 
@@ -130,7 +134,7 @@
     coupling = jnp.concatenate([top_layer, rest_layers], axis=0)
     permittivity = lookup(regions, eps_table)
     shift_scalar = shift_value[0]
-    padded_basis = padded(krylov_basis, (("row", 2), ("col", 3)), 1)
+    padded_basis = padded(krylov_basis, (("row", 2, 0), ("col", 3, 1)), 1)
     image_basis = operator_block(padded_basis, coupling, permittivity, shift_scalar)
     image_flat = image_basis.reshape(columns, -1)
     partial = jnp.stack(

time: 64.8 us -> 63.2 us (0.975)
  waiting for transfers between devices: 16.9 us -> 11.8 us
  starting transfers between devices: 23.9 us -> 25.3 us
  matrix products: 3.08 us -> 4.18 us
  local copies, waits for them, and re-layouts: 5.43 us -> 6.18 us
    ppermute x2, waiting for transfers between devices: 8.2 us -> 4.67 us  [padded(): before = lax.ppermute(last, axis, up)]
    ppermute x2, starting transfers between devices: 6.2 us -> 7.95 us  [padded(): before = lax.ppermute(last, axis, up)]
    ppermute x2, waiting for transfers between devices: 1.58 us -> 0.01 us  [padded(): lax.ppermute(jnp.concatenate([leading[:, c:c + 1] for c in kept], axis=1)...]
    dot_general x3, matrix products: 1.73 us -> 2.84 us  [inner_products(): jnp.dot(left, right.T, precision=lax.Precision.HIGHEST, preferred_element...]
    unnamed x8 -> x6, local copies, waits for them, and re-layouts: 3.85 us -> 4.53 us
  transfers between devices with their start and end apart: 10 -> 10, of which waited for: 6 -> 6; matrix products, arithmetic and copies ran while one was open for 4% -> 6% of each run, Pallas kernels for 0% -> 0%
where the time goes in v5:
time: 63.2 us; the launch traced here: 62.8 us
  starting transfers between devices  25.3 us (40%)
  other arithmetic  13.7 us (22%)
  waiting for transfers between devices  11.8 us (19%)
  local copies, waits for them, and re-layouts  6.18 us (10%)
  matrix products  4.18 us (7%)
  between operations  1.62 us (3%)
    ppermute x4, starting transfers between devices, butterfly_sum(): x = x + lax.ppermute(x, axes, [(i, i ^ step) for i in range(peers)])  8.94 us
    ppermute x2, starting transfers between devices, padded(): before = lax.ppermute(last, axis, up)  7.95 us
    ppermute x4, waiting for transfers between devices, butterfly_sum(): x = x + lax.ppermute(x, axes, [(i, i ^ step) for i in range(peers)])  7.12 us
    another operation x3, other arithmetic, factor_inverse(): lower_factor = jnp.linalg.cholesky(gram_matrix)  6.52 us
    ppermute x2, starting transfers between devices, shifted(): return lax.ppermute(x, axis, pairs)  5.84 us
    another operation x1, other arithmetic, factor_inverse(): lax.linalg.triangular_solve(lower_factor, jnp.eye(gram_matrix.shape[0], d...  4.9 us
    ppermute x2, waiting for transfers between devices, padded(): before = lax.ppermute(last, axis, up)  4.67 us
    unnamed x6, local copies, waits for them, and re-layouts  4.53 us
  transfers between devices with their start and end apart: 10, of which 6 were waited for; matrix products, arithmetic and copies ran while one was open for 6% of the time, Pallas kernels for 0%

profile of v5, /device:TPU:0, one launch (start us, length us, event | category | flops | bytes accessed | tf_op | source)
XLA Modules:
  0.0 62.8 jit_solution(3712388636950068543)
XLA Ops:
  0.6 1.0 %copy.71 = f32[64,3,1,4,128]{4,0,3,2,1:T(8,128)S(1)} copy(f32[64,3,1,4,128]{4,3,2,1,0:T(4,128)} %param.5) | data formatting | bytes 786432 | tf_op args[0]
  1.7 4.9 %collective-permute-start.2 = (f32[64,3,1,4,128]{4,0,3,2,1:T(8,128)S(1)}, f32[64,3,1,4,128]{4,0,3,2,1:T(8,128)S(1)}, u32[]{:S(2)}, u32[]{:S(2)}) collective-permute-start(f32[64,3,1,4,128]{4,0,3,2,1:T(8,128)S(1)} %copy.71), channel_id=1, source_target_pairs={{0,2},{2,4},{4,6},{6,8},{8,10},{10,12},{12,14},{1,3},{3,5},{5,7},{... | collective-permute-start | bytes 1179656 | tf_op jit(solution)/shard_map/ppermute | solution.py:21
  6.6 1.3 %collective-permute-start.3 = (f32[64,2,1,4,128]{4,0,3,2,1:T(8,128)S(1)}, f32[64,2,1,4,128]{4,0,3,2,1:T(8,128)S(1)}, u32[]{:S(2)}, u32[]{:S(2)}) collective-permute-start(f32[64,2,1,4,128]{4,0,3,2,1:T(8,128)S(1)} %concatenate.37), channel_id=1, source_target_pairs={{2,0},{4,2},{6,4},{8,6},{10,8},{12,10},{14,12},{3,1},{5,3},{7,5},{... | collective-permute-start | bytes 786440 | tf_op jit(solution)/shard_map/ppermute | solution.py:22
  7.9 0.8 %select_reduce_fusion.1 = (f32[4,128]{1,0:T(4,128)S(1)}, f32[4,128]{1,0:T(4,128)S(1)}) fusion(f32[8]{0:T(128)} %param.8, s32[4,128]{1,0:T(4,128)} %bitcast.89, f32[8]{0:T(128)} %param.7), kind=kLoop, calls=%fused_computation.62 | loop fusion | flops 19456 | bytes 6208 | tf_op jit(solution)/shard_map/reduce_sum | solution.py:84
  8.7 4.5 %collective-permute-start = (f32[1,4,128]{2,1,0:T(4,128)S(1)}, f32[1,4,128]{2,1,0:T(4,128)S(1)}, u32[]{:S(2)}, u32[]{:S(2)}) collective-permute-start(f32[1,4,128]{2,1,0:T(4,128)S(1)} %bitcast.86), channel_id=1, source_target_pairs={{0,2},{2,4},{4,6},{6,8},{8,10},{10,12},{12,14},{1,3},{3,5},{5,7},{... | collective-permute-start | bytes 6152 | tf_op jit(solution)/shard_map/ppermute | solution.py:10
  13.2 1.3 %collective-permute-start.1 = (f32[1,1,128]{2,1,0:T(1,128)S(1)}, f32[1,1,128]{2,1,0:T(1,128)S(1)}, u32[]{:S(2)}, u32[]{:S(2)}) collective-permute-start(f32[1,1,128]{2,1,0:T(1,128)S(1)} %slice.110), channel_id=1, source_target_pairs={{0,1},{2,3},{4,5},{6,7},{8,9},{10,11},{12,13},{14,15},{16,17},{18,... | collective-permute-start | bytes 1544 | tf_op jit(solution)/shard_map/ppermute | solution.py:10
  14.5 1.6 %fusion.3 = f32[1,64,64]{2,1,0:T(8,128)S(1)} fusion(f32[64,3,4,128]{3,2,1,0:T(4,128)} %bitcast.82), kind=kOutput, calls=%fused_computation.8 | convolution fusion | flops 75501568 | bytes 409600 | tf_op jit(solution)/shard_map/dot_general | solution.py:99
  17.0 3.6 %collective-permute-done.2 = f32[64,3,1,4,128]{4,0,3,2,1:T(8,128)S(1)} collective-permute-done((f32[64,3,1,4,128]{4,0,3,2,1:T(8,128)S(1)}, f32[64,3,1,4,128]{4,0,3,2,1:T(8,128)S(1)}, u32[]{:S(2)}, u32[]{:S(2)}) %collective-permute-start.2) | collective-permute-done | bytes 393248 | tf_op jit(solution)/shard_map/ppermute | solution.py:21
  20.6 1.3 %collective-permute-start.5 = (f32[64,2,3,1,128]{4,0,3,2,1:T(8,128)S(1)}, f32[64,2,3,1,128]{4,0,3,2,1:T(8,128)S(1)}, u32[]{:S(2)}, u32[]{:S(2)}) collective-permute-start(f32[64,2,3,1,128]{4,0,3,2,1:T(8,128)S(1)} %fusion.15), channel_id=1, source_target_pairs={{1,0},{3,2},{5,4},{7,6},{9,8},{11,10},{13,12},{15,14},{17,16},{19,... | collective-permute-start | bytes 589832 | tf_op jit(solution)/shard_map/ppermute | solution.py:22
  21.9 3.1 %collective-permute-start.4 = (f32[64,3,3,1,128]{4,0,3,2,1:T(8,128)S(1)}, f32[64,3,3,1,128]{4,0,3,2,1:T(8,128)S(1)}, u32[]{:S(2)}, u32[]{:S(2)}) collective-permute-start(f32[64,3,3,1,128]{4,0,3,2,1:T(8,128)S(1)} %pad_maximum_fusion), channel_id=1, source_target_pairs={{0,1},{2,3},{4,5},{6,7},{8,9},{10,11},{12,13},{14,15},{16,17},{18,... | collective-permute-start | bytes 884744 | tf_op jit(solution)/shard_map/ppermute | solution.py:21
  25.0 1.1 %collective-permute-done.4 = f32[64,3,3,1,128]{4,0,3,2,1:T(8,128)S(1)} collective-permute-done((f32[64,3,3,1,128]{4,0,3,2,1:T(8,128)S(1)}, f32[64,3,3,1,128]{4,0,3,2,1:T(8,128)S(1)}, u32[]{:S(2)}, u32[]{:S(2)}) %collective-permute-start.4) | collective-permute-done | bytes 294944 | tf_op jit(solution)/shard_map/ppermute | solution.py:21
  27.4 0.8 %copy-done = f32[64,3,1,4,128]{4,3,2,1,0:T(4,128)S(1)} copy-done((f32[64,3,1,4,128]{4,3,2,1,0:T(4,128)S(1)}, f32[64,3,1,4,128]{4,3,2,1,0:T(4,128)}, u32[]{:S(2)}) %copy-start) | copy-done | bytes 393240
  29.2 0.9 %collective-permute-done.6 = f32[2,64,64]{1,2,0:T(8,128)S(1)} collective-permute-done((f32[2,64,64]{1,2,0:T(8,128)S(1)}, f32[2,64,64]{1,2,0:T(8,128)S(1)}, u32[]{:S(2)}, u32[]{:S(2)}) %collective-permute-start.6) | collective-permute-done | bytes 32800 | tf_op jit(solution)/shard_map/ppermute | solution.py:93
  30.1 2.5 %collective-permute-start.7 = (f32[2,64,64]{1,2,0:T(8,128)S(1)}, f32[2,64,64]{1,2,0:T(8,128)S(1)}, u32[]{:S(2)}, u32[]{:S(2)}) collective-permute-start(f32[2,64,64]{1,2,0:T(8,128)S(1)} %fusion.29), channel_id=1, source_target_pairs={{0,2},{1,3},{2,0},{3,1},{4,6},{5,7},{6,4},{7,5},{8,10},{9,11},{10,... | collective-permute-start | bytes 98312 | tf_op jit(solution)/shard_map/ppermute | solution.py:93
  32.6 2.6 %collective-permute-done.7 = f32[2,64,64]{1,2,0:T(8,128)S(1)} collective-permute-done((f32[2,64,64]{1,2,0:T(8,128)S(1)}, f32[2,64,64]{1,2,0:T(8,128)S(1)}, u32[]{:S(2)}, u32[]{:S(2)}) %collective-permute-start.7) | collective-permute-done | bytes 32800 | tf_op jit(solution)/shard_map/ppermute | solution.py:93
  35.3 2.9 %collective-permute-start.8 = (f32[2,64,64]{1,2,0:T(8,128)S(1)}, f32[2,64,64]{1,2,0:T(8,128)S(1)}, u32[]{:S(2)}, u32[]{:S(2)}) collective-permute-start(f32[2,64,64]{1,2,0:T(8,128)S(1)} %fusion.35), channel_id=1, source_target_pairs={{0,4},{1,5},{2,6},{3,7},{4,0},{5,1},{6,2},{7,3},{8,12},{9,13},{10,... | collective-permute-start | bytes 98312 | tf_op jit(solution)/shard_map/ppermute | solution.py:93
  38.1 2.2 %collective-permute-done.8 = f32[2,64,64]{1,2,0:T(8,128)S(1)} collective-permute-done((f32[2,64,64]{1,2,0:T(8,128)S(1)}, f32[2,64,64]{1,2,0:T(8,128)S(1)}, u32[]{:S(2)}, u32[]{:S(2)}) %collective-permute-start.8) | collective-permute-done | bytes 32800 | tf_op jit(solution)/shard_map/ppermute | solution.py:93
  40.4 3.1 %collective-permute-start.9 = (f32[2,64,64]{1,2,0:T(8,128)S(1)}, f32[2,64,64]{1,2,0:T(8,128)S(1)}, u32[]{:S(2)}, u32[]{:S(2)}) collective-permute-start(f32[2,64,64]{1,2,0:T(8,128)S(1)} %add.37), channel_id=1, source_target_pairs={{0,8},{1,9},{2,10},{3,11},{4,12},{5,13},{6,14},{7,15},{8,0},{9,1},... | collective-permute-start | bytes 98312 | tf_op jit(solution)/shard_map/ppermute | solution.py:93
  44.4 1.4 %collective-permute-done.9 = f32[2,64,64]{1,2,0:T(8,128)S(1)} collective-permute-done((f32[2,64,64]{1,2,0:T(8,128)S(1)}, f32[2,64,64]{1,2,0:T(8,128)S(1)}, u32[]{:S(2)}, u32[]{:S(2)}) %collective-permute-start.9) | collective-permute-done | bytes 32800 | tf_op jit(solution)/shard_map/ppermute | solution.py:93
  45.8 5.8 %cholesky.17 = f32[64,64]{1,0:T(8,128)S(1)} custom-call(f32[64,64]{1,0:T(8,128)S(1)} %fusion.23), custom_call_target="Cholesky" | custom-call | tf_op jit(solution)/shard_map/jit(cholesky)/cholesky | solution.py:116
  53.0 4.9 %custom-call.6 = f32[1,64,64]{1,2,0:T(8,128)S(1)} custom-call(f32[1,64,64]{2,1,0:T(8,128)S(1)} %get-tuple-element.34), custom_call_target="InvertDiagBlocksLowerTriangular" | custom-call | tf_op jit(solution)/shard_map/triangular_solve | solution.py:117
  58.3 0.8 %fusion.31 = f32[64,64]{1,0:T(8,128)} fusion(f32[64,64]{1,0:T(8,128)S(1)} %fusion.22, f32[64,64]{1,0:T(8,128)S(1)} %fusion.26), kind=kOutput, calls=%fused_computation.71 | convolution fusion | flops 3145728 | bytes 49152 | tf_op jit(solution)/shard_map/dot_general | solution.py:99
  59.6 1.0 %copy.83 = f32[64,3,1,4,128]{4,3,2,1,0:T(4,128)} copy(f32[64,3,1,4,128]{4,0,3,1,2:T(8,128)S(1)} %convolution_bitcast_fusion) | data formatting | bytes 786432
  61.1 1.0 %copy.81 = f32[64,3,1,4,128]{4,3,2,1,0:T(4,128)} copy(f32[64,3,1,4,128]{4,0,3,1,2:T(8,128)S(1)} %convolution_bitcast_fusion.1) | data formatting | bytes 786432
  (47 shorter events, 6.8 us)
Async XLA Ops:
  1.7 18.9 %collective-permute-start.2 = (f32[64,3,1,4,128]{4,0,3,2,1:T(8,128)S(1)}, f32[64,3,1,4,128]{4,0,3,2,1:T(8,128)S(1)}, u32[]{:S(2)}, u32[]{:S(2)}) collective-permute-start(f32[64,3,1,4,128]{4,0,3,2,1:T(8,128)S(1)} %copy.71), channel_id=1, source_target_pairs={{0,2},{2,4},{4,6},{6,8},{8,10},{10,12},{12,14},{1,3},{3,5},{5,7},{... | collective-permute-start | bytes 1179656 | tf_op jit(solution)/shard_map/ppermute | solution.py:21
  6.6 10.3 %collective-permute-start.3 = (f32[64,2,1,4,128]{4,0,3,2,1:T(8,128)S(1)}, f32[64,2,1,4,128]{4,0,3,2,1:T(8,128)S(1)}, u32[]{:S(2)}, u32[]{:S(2)}) collective-permute-start(f32[64,2,1,4,128]{4,0,3,2,1:T(8,128)S(1)} %concatenate.37), channel_id=1, source_target_pairs={{2,0},{4,2},{6,4},{8,6},{10,8},{12,10},{14,12},{3,1},{5,3},{7,5},{... | collective-permute-start | bytes 786440 | tf_op jit(solution)/shard_map/ppermute | solution.py:22
  8.7 16.3 %collective-permute-start = (f32[1,4,128]{2,1,0:T(4,128)S(1)}, f32[1,4,128]{2,1,0:T(4,128)S(1)}, u32[]{:S(2)}, u32[]{:S(2)}) collective-permute-start(f32[1,4,128]{2,1,0:T(4,128)S(1)} %bitcast.86), channel_id=1, source_target_pairs={{0,2},{2,4},{4,6},{6,8},{8,10},{10,12},{12,14},{1,3},{3,5},{5,7},{... | collective-permute-start | bytes 6152 | tf_op jit(solution)/shard_map/ppermute | solution.py:10
  13.2 11.7 %collective-permute-start.1 = (f32[1,1,128]{2,1,0:T(1,128)S(1)}, f32[1,1,128]{2,1,0:T(1,128)S(1)}, u32[]{:S(2)}, u32[]{:S(2)}) collective-permute-start(f32[1,1,128]{2,1,0:T(1,128)S(1)} %slice.110), channel_id=1, source_target_pairs={{0,1},{2,3},{4,5},{6,7},{8,9},{10,11},{12,13},{14,15},{16,17},{18,... | collective-permute-start | bytes 1544 | tf_op jit(solution)/shard_map/ppermute | solution.py:10
  20.6 4.4 %collective-permute-start.5 = (f32[64,2,3,1,128]{4,0,3,2,1:T(8,128)S(1)}, f32[64,2,3,1,128]{4,0,3,2,1:T(8,128)S(1)}, u32[]{:S(2)}, u32[]{:S(2)}) collective-permute-start(f32[64,2,3,1,128]{4,0,3,2,1:T(8,128)S(1)} %fusion.15), channel_id=1, source_target_pairs={{1,0},{3,2},{5,4},{7,6},{9,8},{11,10},{13,12},{15,14},{17,16},{19,... | collective-permute-start | bytes 589832 | tf_op jit(solution)/shard_map/ppermute | solution.py:22
  21.9 4.2 %collective-permute-start.4 = (f32[64,3,3,1,128]{4,0,3,2,1:T(8,128)S(1)}, f32[64,3,3,1,128]{4,0,3,2,1:T(8,128)S(1)}, u32[]{:S(2)}, u32[]{:S(2)}) collective-permute-start(f32[64,3,3,1,128]{4,0,3,2,1:T(8,128)S(1)} %pad_maximum_fusion), channel_id=1, source_target_pairs={{0,1},{2,3},{4,5},{6,7},{8,9},{10,11},{12,13},{14,15},{16,17},{18,... | collective-permute-start | bytes 884744 | tf_op jit(solution)/shard_map/ppermute | solution.py:21
  27.2 1.0 %copy-start = (f32[64,3,1,4,128]{4,3,2,1,0:T(4,128)S(1)}, f32[64,3,1,4,128]{4,3,2,1,0:T(4,128)}, u32[]{:S(2)}) copy-start(f32[64,3,1,4,128]{4,3,2,1,0:T(4,128)} %param.5) | copy-start | bytes 1179652
  28.7 1.3 %collective-permute-start.6 = (f32[2,64,64]{1,2,0:T(8,128)S(1)}, f32[2,64,64]{1,2,0:T(8,128)S(1)}, u32[]{:S(2)}, u32[]{:S(2)}) collective-permute-start(f32[2,64,64]{1,2,0:T(8,128)S(1)} %pad_maximum_fusion.1), channel_id=1, source_target_pairs={{0,1},{1,0},{2,3},{3,2},{4,5},{5,4},{6,7},{7,6},{8,9},{9,8},{10,11... | collective-permute-start | bytes 98312 | tf_op jit(solution)/shard_map/ppermute | solution.py:93
  30.1 5.2 %collective-permute-start.7 = (f32[2,64,64]{1,2,0:T(8,128)S(1)}, f32[2,64,64]{1,2,0:T(8,128)S(1)}, u32[]{:S(2)}, u32[]{:S(2)}) collective-permute-start(f32[2,64,64]{1,2,0:T(8,128)S(1)} %fusion.29), channel_id=1, source_target_pairs={{0,2},{1,3},{2,0},{3,1},{4,6},{5,7},{6,4},{7,5},{8,10},{9,11},{10,... | collective-permute-start | bytes 98312 | tf_op jit(solution)/shard_map/ppermute | solution.py:93
  35.3 5.1 %collective-permute-start.8 = (f32[2,64,64]{1,2,0:T(8,128)S(1)}, f32[2,64,64]{1,2,0:T(8,128)S(1)}, u32[]{:S(2)}, u32[]{:S(2)}) collective-permute-start(f32[2,64,64]{1,2,0:T(8,128)S(1)} %fusion.35), channel_id=1, source_target_pairs={{0,4},{1,5},{2,6},{3,7},{4,0},{5,1},{6,2},{7,3},{8,12},{9,13},{10,... | collective-permute-start | bytes 98312 | tf_op jit(solution)/shard_map/ppermute | solution.py:93
  40.4 5.3 %collective-permute-start.9 = (f32[2,64,64]{1,2,0:T(8,128)S(1)}, f32[2,64,64]{1,2,0:T(8,128)S(1)}, u32[]{:S(2)}, u32[]{:S(2)}) collective-permute-start(f32[2,64,64]{1,2,0:T(8,128)S(1)} %add.37), channel_id=1, source_target_pairs={{0,8},{1,9},{2,10},{3,11},{4,12},{5,13},{6,14},{7,15},{8,0},{9,1},... | collective-permute-start | bytes 98312 | tf_op jit(solution)/shard_map/ppermute | solution.py:93

commit v6 on v5

--- a/solution.py
+++ b/solution.py
@@ -11,20 +11,24 @@
 
 
 def padded(x, sides, width):
-    for axis, dim, unused in sides:
+    riders = []
+    for axis, dim, unused, rider in sides:
         peers, length = (lax.axis_size(axis), x.shape[dim])
         up = [(i, (i + 1) % peers) for i in range(peers - 1)]
         down = [(j, i) for i, j in up]
         last = lax.slice_in_dim(x, length - width, length, axis=dim)
         leading = lax.slice_in_dim(x, 0, width, axis=dim)
         kept = [c for c in range(x.shape[1]) if c != unused]
-        before = lax.ppermute(last, axis, up)
+        carried = jnp.broadcast_to(rider, (1,) + last.shape[1:])
+        received = lax.ppermute(jnp.concatenate([last, carried], axis=0), axis, up)
+        before = received[: x.shape[0]]
+        riders.append(received[x.shape[0] :])
         sent = lax.ppermute(jnp.concatenate([leading[:, c : c + 1] for c in kept], axis=1), axis, down)
         parts = [sent[:, i : i + 1] for i in range(len(kept))]
         parts.insert(unused, jnp.zeros_like(parts[0]))
         after = jnp.concatenate(parts, axis=1)
         x = jnp.concatenate([before, x, after], axis=dim)
-    return x
+    return x, riders
 
 
 def forward_z(values):
@@ -126,15 +130,19 @@
     total_rows = flattened.shape[1] * lax.axis_size("row") * lax.axis_size("col")
     cells_y = regions.shape[1]
     local_mu = lookup(regions, mu_table)
-    from_lower_row = shifted(local_mu, "row", 1)
-    from_lower_col = shifted(local_mu[:, cells_y - 1 :], "col", 1)
+    padded_basis, (row_rider, col_rider) = padded(
+        krylov_basis,
+        (("row", 2, 0, local_mu[None, None]), ("col", 3, 1, local_mu[None, None, :, cells_y - 1 :])),
+        1,
+    )
+    from_lower_row = row_rider[0, 0]
+    from_lower_col = col_rider[0, 0, :1]
     corner_zero = jnp.zeros((1, 1, local_mu.shape[2]), jnp.float32)
     top_layer = jnp.concatenate([corner_zero, from_lower_row], axis=1)
     rest_layers = jnp.concatenate([from_lower_col, local_mu], axis=1)
     coupling = jnp.concatenate([top_layer, rest_layers], axis=0)
     permittivity = lookup(regions, eps_table)
     shift_scalar = shift_value[0]
-    padded_basis = padded(krylov_basis, (("row", 2, 0), ("col", 3, 1)), 1)
     image_basis = operator_block(padded_basis, coupling, permittivity, shift_scalar)
     image_flat = image_basis.reshape(columns, -1)
     partial = jnp.stack(

time: 63.2 us -> 63.5 us (level)
  waiting for transfers between devices: 11.8 us -> 20.9 us
  starting transfers between devices: 25.3 us -> 18.5 us
  matrix products: 4.18 us -> 3.07 us
  local copies, waits for them, and re-layouts: 6.18 us -> 5.45 us
    ppermute x4 -> x2, waiting for transfers between devices: 4.68 us -> 10.1 us  [padded(): received = lax.ppermute(jnp.concatenate([last, carried], axis=0), axis, up)]
    ppermute x4 -> x2, starting transfers between devices: 13.8 us -> 8.59 us  [padded(): received = lax.ppermute(jnp.concatenate([last, carried], axis=0), axis, up)]
    ppermute x2, waiting for transfers between devices: 0.01 us -> 2.84 us  [padded(): lax.ppermute(jnp.concatenate([leading[:, c:c + 1] for c in kept], axis=1)...]
    ppermute x4, starting transfers between devices: 8.94 us -> 7.28 us  [butterfly_sum(): x = x + lax.ppermute(x, axes, [(i, i ^ step) for i in range(peers)])]
    dot_general x3, matrix products: 2.84 us -> 1.72 us  [inner_products(): jnp.dot(left, right.T, precision=lax.Precision.HIGHEST, preferred_element...]
    unnamed x6, local copies, waits for them, and re-layouts: 4.53 us -> 3.73 us
    ppermute x4, waiting for transfers between devices: 7.12 us -> 7.9 us  [butterfly_sum(): x = x + lax.ppermute(x, axes, [(i, i ^ step) for i in range(peers)])]
  transfers between devices with their start and end apart: 10 -> 8, of which waited for: 6 -> 7; matrix products, arithmetic and copies ran while one was open for 6% -> 4% of each run, Pallas kernels for 0% -> 0%
where the time goes in v6:
time: 63.5 us; the launch traced here: 63.2 us
  waiting for transfers between devices  20.9 us (33%)
  starting transfers between devices  18.5 us (29%)
  other arithmetic  13.7 us (22%)
  local copies, waits for them, and re-layouts  5.45 us (9%)
  matrix products  3.07 us (5%)
  between operations  1.64 us (3%)
    ppermute x2, waiting for transfers between devices, padded(): received = lax.ppermute(jnp.concatenate([last, carried], axis=0), axis, up)  10.1 us
    ppermute x2, starting transfers between devices, padded(): received = lax.ppermute(jnp.concatenate([last, carried], axis=0), axis, up)  8.59 us
    ppermute x4, waiting for transfers between devices, butterfly_sum(): x = x + lax.ppermute(x, axes, [(i, i ^ step) for i in range(peers)])  7.9 us
    ppermute x4, starting transfers between devices, butterfly_sum(): x = x + lax.ppermute(x, axes, [(i, i ^ step) for i in range(peers)])  7.28 us
    another operation x3, other arithmetic, factor_inverse(): lower_factor = jnp.linalg.cholesky(gram_matrix)  6.52 us
    another operation x1, other arithmetic, factor_inverse(): lax.linalg.triangular_solve(lower_factor, jnp.eye(gram_matrix.shape[0], d...  4.89 us
    unnamed x6, local copies, waits for them, and re-layouts  3.73 us
    ppermute x2, waiting for transfers between devices, padded(): lax.ppermute(jnp.concatenate([leading[:, c:c + 1] for c in kept], axis=1)...  2.84 us
  transfers between devices with their start and end apart: 8, of which 7 were waited for; matrix products, arithmetic and copies ran while one was open for 4% of the time, Pallas kernels for 0%

profile of v6, /device:TPU:0, one launch (start us, length us, event | category | flops | bytes accessed | tf_op | source)
XLA Modules:
  0.0 63.2 jit_solution(16204650609586960436)
XLA Ops:
  0.6 1.0 %copy.100 = f32[64,3,1,4,128]{4,0,3,2,1:T(8,128)S(1)} copy(f32[64,3,1,4,128]{4,3,2,1,0:T(4,128)} %param.5) | data formatting | bytes 786432 | tf_op args[0]
  1.7 1.3 %collective-permute-start.1 = (f32[64,2,1,4,128]{4,0,3,2,1:T(8,128)S(1)}, f32[64,2,1,4,128]{4,0,3,2,1:T(8,128)S(1)}, u32[]{:S(2)}, u32[]{:S(2)}) collective-permute-start(f32[64,2,1,4,128]{4,0,3,2,1:T(8,128)S(1)} %concatenate.45), channel_id=1, source_target_pairs={{2,0},{4,2},{6,4},{8,6},{10,8},{12,10},{14,12},{3,1},{5,3},{7,5},{... | collective-permute-start | bytes 786440 | tf_op jit(solution)/shard_map/ppermute | solution.py:26
  3.0 0.8 %select_reduce_fusion.1 = (f32[4,128]{1,0:T(4,128)S(1)}, f32[4,128]{1,0:T(4,128)S(1)}) fusion(f32[8]{0:T(128)} %param.8, s32[4,128]{1,0:T(4,128)} %bitcast.94, f32[8]{0:T(128)} %param.7), kind=kLoop, calls=%fused_computation.65 | loop fusion | flops 19456 | bytes 6208 | tf_op jit(solution)/shard_map/reduce_sum | solution.py:88
  3.8 5.5 %collective-permute-start = (f32[65,3,1,4,128]{4,0,3,2,1:T(8,128)S(1)}, f32[65,3,1,4,128]{4,0,3,2,1:T(8,128)S(1)}, u32[]{:S(2)}, u32[]{:S(2)}) collective-permute-start(f32[65,3,1,4,128]{4,0,3,2,1:T(8,128)S(1)} %pad_maximum_fusion), channel_id=1, source_target_pairs={{0,2},{2,4},{4,6},{6,8},{8,10},{10,12},{12,14},{1,3},{3,5},{5,7},{... | collective-permute-start | bytes 1198088 | tf_op jit(solution)/shard_map/ppermute | solution.py:23
  10.0 2.8 %collective-permute-done.1 = f32[64,2,1,4,128]{4,0,3,2,1:T(8,128)S(1)} collective-permute-done((f32[64,2,1,4,128]{4,0,3,2,1:T(8,128)S(1)}, f32[64,2,1,4,128]{4,0,3,2,1:T(8,128)S(1)}, u32[]{:S(2)}, u32[]{:S(2)}) %collective-permute-start.1) | collective-permute-done | bytes 262176 | tf_op jit(solution)/shard_map/ppermute | solution.py:26
  12.9 9.6 %collective-permute-done = f32[65,3,1,4,128]{4,0,3,2,1:T(8,128)S(1)} collective-permute-done((f32[65,3,1,4,128]{4,0,3,2,1:T(8,128)S(1)}, f32[65,3,1,4,128]{4,0,3,2,1:T(8,128)S(1)}, u32[]{:S(2)}, u32[]{:S(2)}) %collective-permute-start) | collective-permute-done | bytes 399392 | tf_op jit(solution)/shard_map/ppermute | solution.py:23
  22.6 1.3 %collective-permute-start.3 = (f32[64,2,3,1,128]{4,0,3,2,1:T(8,128)S(1)}, f32[64,2,3,1,128]{4,0,3,2,1:T(8,128)S(1)}, u32[]{:S(2)}, u32[]{:S(2)}) collective-permute-start(f32[64,2,3,1,128]{4,0,3,2,1:T(8,128)S(1)} %fusion.16), channel_id=1, source_target_pairs={{1,0},{3,2},{5,4},{7,6},{9,8},{11,10},{13,12},{15,14},{17,16},{19,... | collective-permute-start | bytes 589832 | tf_op jit(solution)/shard_map/ppermute | solution.py:26
  23.9 3.1 %collective-permute-start.2 = (f32[65,3,3,1,128]{4,0,3,2,1:T(8,128)S(1)}, f32[65,3,3,1,128]{4,0,3,2,1:T(8,128)S(1)}, u32[]{:S(2)}, u32[]{:S(2)}) collective-permute-start(f32[65,3,3,1,128]{4,0,3,2,1:T(8,128)S(1)} %fusion.9), channel_id=1, source_target_pairs={{0,1},{2,3},{4,5},{6,7},{8,9},{10,11},{12,13},{14,15},{16,17},{18,... | collective-permute-start | bytes 898568 | tf_op jit(solution)/shard_map/ppermute | solution.py:23
  27.6 0.6 collective-permute-done.2
  30.5 0.9 %collective-permute-done.4 = f32[2,64,64]{1,2,0:T(8,128)S(1)} collective-permute-done((f32[2,64,64]{1,2,0:T(8,128)S(1)}, f32[2,64,64]{1,2,0:T(8,128)S(1)}, u32[]{:S(2)}, u32[]{:S(2)}) %collective-permute-start.4) | collective-permute-done | bytes 32800 | tf_op jit(solution)/shard_map/ppermute | solution.py:97
  31.4 2.5 %collective-permute-start.5 = (f32[2,64,64]{1,2,0:T(8,128)S(1)}, f32[2,64,64]{1,2,0:T(8,128)S(1)}, u32[]{:S(2)}, u32[]{:S(2)}) collective-permute-start(f32[2,64,64]{1,2,0:T(8,128)S(1)} %fusion.30), channel_id=1, source_target_pairs={{0,2},{1,3},{2,0},{3,1},{4,6},{5,7},{6,4},{7,5},{8,10},{9,11},{10,... | collective-permute-start | bytes 98312 | tf_op jit(solution)/shard_map/ppermute | solution.py:97
  33.9 2.6 %collective-permute-done.5 = f32[2,64,64]{1,2,0:T(8,128)S(1)} collective-permute-done((f32[2,64,64]{1,2,0:T(8,128)S(1)}, f32[2,64,64]{1,2,0:T(8,128)S(1)}, u32[]{:S(2)}, u32[]{:S(2)}) %collective-permute-start.5) | collective-permute-done | bytes 32800 | tf_op jit(solution)/shard_map/ppermute | solution.py:97
  36.6 1.6 %collective-permute-start.6 = (f32[2,64,64]{1,2,0:T(8,128)S(1)}, f32[2,64,64]{1,2,0:T(8,128)S(1)}, u32[]{:S(2)}, u32[]{:S(2)}) collective-permute-start(f32[2,64,64]{1,2,0:T(8,128)S(1)} %fusion.36), channel_id=1, source_target_pairs={{0,4},{1,5},{2,6},{3,7},{4,0},{5,1},{6,2},{7,3},{8,12},{9,13},{10,... | collective-permute-start | bytes 98312 | tf_op jit(solution)/shard_map/ppermute | solution.py:97
  38.2 2.7 %collective-permute-done.6 = f32[2,64,64]{1,2,0:T(8,128)S(1)} collective-permute-done((f32[2,64,64]{1,2,0:T(8,128)S(1)}, f32[2,64,64]{1,2,0:T(8,128)S(1)}, u32[]{:S(2)}, u32[]{:S(2)}) %collective-permute-start.6) | collective-permute-done | bytes 32800 | tf_op jit(solution)/shard_map/ppermute | solution.py:97
  40.9 2.7 %collective-permute-start.7 = (f32[2,64,64]{1,2,0:T(8,128)S(1)}, f32[2,64,64]{1,2,0:T(8,128)S(1)}, u32[]{:S(2)}, u32[]{:S(2)}) collective-permute-start(f32[2,64,64]{1,2,0:T(8,128)S(1)} %add.37), channel_id=1, source_target_pairs={{0,8},{1,9},{2,10},{3,11},{4,12},{5,13},{6,14},{7,15},{8,0},{9,1},... | collective-permute-start | bytes 98312 | tf_op jit(solution)/shard_map/ppermute | solution.py:97
  44.4 1.7 %collective-permute-done.7 = f32[2,64,64]{1,2,0:T(8,128)S(1)} collective-permute-done((f32[2,64,64]{1,2,0:T(8,128)S(1)}, f32[2,64,64]{1,2,0:T(8,128)S(1)}, u32[]{:S(2)}, u32[]{:S(2)}) %collective-permute-start.7) | collective-permute-done | bytes 32800 | tf_op jit(solution)/shard_map/ppermute | solution.py:97
  46.2 5.8 %cholesky.17 = f32[64,64]{1,0:T(8,128)S(1)} custom-call(f32[64,64]{1,0:T(8,128)S(1)} %fusion.24), custom_call_target="Cholesky" | custom-call | tf_op jit(solution)/shard_map/jit(cholesky)/cholesky | solution.py:120
  52.1 0.6 %compare_reduce_fusion = pred[]{:T(512)} fusion(f32[64]{0:T(128)S(1)} %select_reduce_fusion), kind=kLoop, calls=%fused_computation.70 | loop fusion | flops 127 | bytes 257 | tf_op jit(solution)/shard_map/jit(cholesky)/cholesky | solution.py:120
  52.8 0.7 %fusion.29 = (f32[64,64]{0,1:T(8,128)S(1)}, f32[1,64,64]{2,1,0:T(8,128)S(1)}) fusion(f32[64,64]{1,0:T(8,128)S(1)} %cholesky.17, pred[]{:T(512)} %compare_reduce_fusion), kind=kLoop, calls=%fused_computation.64 | loop fusion | flops 16384 | bytes 49153 | tf_op jit(solution)/shard_map/transpose | solution.py:124
  53.4 0.7 %copy.111 = f32[64,64]{1,0:T(8,128)} copy(f32[64,64]{0,1:T(8,128)S(1)} %get-tuple-element.37) | data formatting | bytes 32768
  54.1 4.9 %custom-call.6 = f32[1,64,64]{1,2,0:T(8,128)S(1)} custom-call(f32[1,64,64]{2,1,0:T(8,128)S(1)} %get-tuple-element.38), custom_call_target="InvertDiagBlocksLowerTriangular" | custom-call | tf_op jit(solution)/shard_map/triangular_solve | solution.py:121
  59.5 0.8 %fusion.32 = f32[64,64]{1,0:T(8,128)} fusion(f32[64,64]{1,0:T(8,128)S(1)} %fusion.23, f32[64,64]{1,0:T(8,128)S(1)} %fusion.27), kind=kOutput, calls=%fused_computation.76 | convolution fusion | flops 3145728 | bytes 49152 | tf_op jit(solution)/shard_map/dot_general | solution.py:103
  61.2 1.0 %copy.110 = f32[64,3,1,4,128]{4,3,2,1,0:T(4,128)} copy(f32[64,3,1,4,128]{4,0,3,1,2:T(8,128)S(1)} %convolution_bitcast_fusion.1) | data formatting | bytes 786432
  62.2 1.0 %copy.112 = f32[64,3,1,4,128]{4,3,2,1,0:T(4,128)} copy(f32[64,3,1,4,128]{4,0,3,1,2:T(8,128)S(1)} %convolution_bitcast_fusion) | data formatting | bytes 786432
  (50 shorter events, 5.3 us)
Async XLA Ops:
  1.7 11.2 %collective-permute-start.1 = (f32[64,2,1,4,128]{4,0,3,2,1:T(8,128)S(1)}, f32[64,2,1,4,128]{4,0,3,2,1:T(8,128)S(1)}, u32[]{:S(2)}, u32[]{:S(2)}) collective-permute-start(f32[64,2,1,4,128]{4,0,3,2,1:T(8,128)S(1)} %concatenate.45), channel_id=1, source_target_pairs={{2,0},{4,2},{6,4},{8,6},{10,8},{12,10},{14,12},{3,1},{5,3},{7,5},{... | collective-permute-start | bytes 786440 | tf_op jit(solution)/shard_map/ppermute | solution.py:26
  3.8 18.7 %collective-permute-start = (f32[65,3,1,4,128]{4,0,3,2,1:T(8,128)S(1)}, f32[65,3,1,4,128]{4,0,3,2,1:T(8,128)S(1)}, u32[]{:S(2)}, u32[]{:S(2)}) collective-permute-start(f32[65,3,1,4,128]{4,0,3,2,1:T(8,128)S(1)} %pad_maximum_fusion), channel_id=1, source_target_pairs={{0,2},{2,4},{4,6},{6,8},{8,10},{10,12},{12,14},{1,3},{3,5},{5,7},{... | collective-permute-start | bytes 1198088 | tf_op jit(solution)/shard_map/ppermute | solution.py:23
  12.9 14.1 %copy-start = (f32[64,3,1,4,128]{4,3,2,1,0:T(4,128)S(1)}, f32[64,3,1,4,128]{4,3,2,1,0:T(4,128)}, u32[]{:S(2)}) copy-start(f32[64,3,1,4,128]{4,3,2,1,0:T(4,128)} %param.5) | copy-start | bytes 1179652
  22.6 5.0 %collective-permute-start.3 = (f32[64,2,3,1,128]{4,0,3,2,1:T(8,128)S(1)}, f32[64,2,3,1,128]{4,0,3,2,1:T(8,128)S(1)}, u32[]{:S(2)}, u32[]{:S(2)}) collective-permute-start(f32[64,2,3,1,128]{4,0,3,2,1:T(8,128)S(1)} %fusion.16), channel_id=1, source_target_pairs={{1,0},{3,2},{5,4},{7,6},{9,8},{11,10},{13,12},{15,14},{17,16},{19,... | collective-permute-start | bytes 589832 | tf_op jit(solution)/shard_map/ppermute | solution.py:26
  23.9 4.3 %collective-permute-start.2 = (f32[65,3,3,1,128]{4,0,3,2,1:T(8,128)S(1)}, f32[65,3,3,1,128]{4,0,3,2,1:T(8,128)S(1)}, u32[]{:S(2)}, u32[]{:S(2)}) collective-permute-start(f32[65,3,3,1,128]{4,0,3,2,1:T(8,128)S(1)} %fusion.9), channel_id=1, source_target_pairs={{0,1},{2,3},{4,5},{6,7},{8,9},{10,11},{12,13},{14,15},{16,17},{18,... | collective-permute-start | bytes 898568 | tf_op jit(solution)/shard_map/ppermute | solution.py:23
  30.0 1.3 %collective-permute-start.4 = (f32[2,64,64]{1,2,0:T(8,128)S(1)}, f32[2,64,64]{1,2,0:T(8,128)S(1)}, u32[]{:S(2)}, u32[]{:S(2)}) collective-permute-start(f32[2,64,64]{1,2,0:T(8,128)S(1)} %pad_maximum_fusion.3), channel_id=1, source_target_pairs={{0,1},{1,0},{2,3},{3,2},{4,5},{5,4},{6,7},{7,6},{8,9},{9,8},{10,11... | collective-permute-start | bytes 98312 | tf_op jit(solution)/shard_map/ppermute | solution.py:97
  31.4 5.2 %collective-permute-start.5 = (f32[2,64,64]{1,2,0:T(8,128)S(1)}, f32[2,64,64]{1,2,0:T(8,128)S(1)}, u32[]{:S(2)}, u32[]{:S(2)}) collective-permute-start(f32[2,64,64]{1,2,0:T(8,128)S(1)} %fusion.30), channel_id=1, source_target_pairs={{0,2},{1,3},{2,0},{3,1},{4,6},{5,7},{6,4},{7,5},{8,10},{9,11},{10,... | collective-permute-start | bytes 98312 | tf_op jit(solution)/shard_map/ppermute | solution.py:97
  36.6 4.3 %collective-permute-start.6 = (f32[2,64,64]{1,2,0:T(8,128)S(1)}, f32[2,64,64]{1,2,0:T(8,128)S(1)}, u32[]{:S(2)}, u32[]{:S(2)}) collective-permute-start(f32[2,64,64]{1,2,0:T(8,128)S(1)} %fusion.36), channel_id=1, source_target_pairs={{0,4},{1,5},{2,6},{3,7},{4,0},{5,1},{6,2},{7,3},{8,12},{9,13},{10,... | collective-permute-start | bytes 98312 | tf_op jit(solution)/shard_map/ppermute | solution.py:97
  40.9 5.2 %collective-permute-start.7 = (f32[2,64,64]{1,2,0:T(8,128)S(1)}, f32[2,64,64]{1,2,0:T(8,128)S(1)}, u32[]{:S(2)}, u32[]{:S(2)}) collective-permute-start(f32[2,64,64]{1,2,0:T(8,128)S(1)} %add.37), channel_id=1, source_target_pairs={{0,8},{1,9},{2,10},{3,11},{4,12},{5,13},{6,14},{7,15},{8,0},{9,1},... | collective-permute-start | bytes 98312 | tf_op jit(solution)/shard_map/ppermute | solution.py:97

commit v7 on v6

--- a/solution.py
+++ b/solution.py
@@ -92,10 +92,9 @@
     peers = 1
     for axis in axes:
         peers *= lax.axis_size(axis)
-    step = 1
-    while step < peers:
+    steps = [1 << b for b in range(peers.bit_length() - 1)]
+    for step in steps[1:][::-1] + steps[:1]:
         x = x + lax.ppermute(x, axes, [(i, i ^ step) for i in range(peers)])
-        step *= 2
     return x
 
 

time: 63.5 us -> 64.6 us (1.017)
  waiting for transfers between devices: 20.9 us -> 23.1 us
  starting transfers between devices: 18.5 us -> 17.3 us
    ppermute x4, waiting for transfers between devices: 7.9 us -> 10.1 us  [butterfly_sum(): x = x + lax.ppermute(x, axes, [(i, i ^ step) for i in range(peers)])]
    ppermute x4, starting transfers between devices: 7.28 us -> 6.14 us  [butterfly_sum(): x = x + lax.ppermute(x, axes, [(i, i ^ step) for i in range(peers)])]
where the time goes in v7:
time: 64.6 us; the launch traced here: 64.3 us
  waiting for transfers between devices  23.1 us (36%)
  starting transfers between devices  17.3 us (27%)
  other arithmetic  13.7 us (21%)
  local copies, waits for them, and re-layouts  5.45 us (8%)
  matrix products  3.08 us (5%)
  between operations  1.65 us (3%)
    ppermute x2, waiting for transfers between devices, padded(): received = lax.ppermute(jnp.concatenate([last, carried], axis=0), axis, up)  10.1 us
    ppermute x4, waiting for transfers between devices, butterfly_sum(): x = x + lax.ppermute(x, axes, [(i, i ^ step) for i in range(peers)])  10.1 us
    ppermute x2, starting transfers between devices, padded(): received = lax.ppermute(jnp.concatenate([last, carried], axis=0), axis, up)  8.59 us
    another operation x3, other arithmetic, factor_inverse(): lower_factor = jnp.linalg.cholesky(gram_matrix)  6.52 us
    ppermute x4, starting transfers between devices, butterfly_sum(): x = x + lax.ppermute(x, axes, [(i, i ^ step) for i in range(peers)])  6.14 us
    another operation x1, other arithmetic, factor_inverse(): lax.linalg.triangular_solve(lower_factor, jnp.eye(gram_matrix.shape[0], d...  4.89 us
    unnamed x6, local copies, waits for them, and re-layouts  3.73 us
    ppermute x2, waiting for transfers between devices, padded(): lax.ppermute(jnp.concatenate([leading[:, c:c + 1] for c in kept], axis=1)...  2.84 us
  transfers between devices with their start and end apart: 8, of which 7 were waited for; matrix products, arithmetic and copies ran while one was open for 4% of the time, Pallas kernels for 0%

profile of v7, /device:TPU:0, one launch (start us, length us, event | category | flops | bytes accessed | tf_op | source)
XLA Modules:
  0.0 64.3 jit_solution(17966938795084095056)
XLA Ops:
  0.6 1.0 %copy.100 = f32[64,3,1,4,128]{4,0,3,2,1:T(8,128)S(1)} copy(f32[64,3,1,4,128]{4,3,2,1,0:T(4,128)} %param.5) | data formatting | bytes 786432 | tf_op args[0]
  1.7 1.3 %collective-permute-start.1 = (f32[64,2,1,4,128]{4,0,3,2,1:T(8,128)S(1)}, f32[64,2,1,4,128]{4,0,3,2,1:T(8,128)S(1)}, u32[]{:S(2)}, u32[]{:S(2)}) collective-permute-start(f32[64,2,1,4,128]{4,0,3,2,1:T(8,128)S(1)} %concatenate.45), channel_id=1, source_target_pairs={{2,0},{4,2},{6,4},{8,6},{10,8},{12,10},{14,12},{3,1},{5,3},{7,5},{... | collective-permute-start | bytes 786440 | tf_op jit(solution)/shard_map/ppermute | solution.py:26
  3.0 0.8 %select_reduce_fusion.1 = (f32[4,128]{1,0:T(4,128)S(1)}, f32[4,128]{1,0:T(4,128)S(1)}) fusion(f32[8]{0:T(128)} %param.8, s32[4,128]{1,0:T(4,128)} %bitcast.94, f32[8]{0:T(128)} %param.7), kind=kLoop, calls=%fused_computation.65 | loop fusion | flops 19456 | bytes 6208 | tf_op jit(solution)/shard_map/reduce_sum | solution.py:88
  3.8 5.5 %collective-permute-start = (f32[65,3,1,4,128]{4,0,3,2,1:T(8,128)S(1)}, f32[65,3,1,4,128]{4,0,3,2,1:T(8,128)S(1)}, u32[]{:S(2)}, u32[]{:S(2)}) collective-permute-start(f32[65,3,1,4,128]{4,0,3,2,1:T(8,128)S(1)} %pad_maximum_fusion), channel_id=1, source_target_pairs={{0,2},{2,4},{4,6},{6,8},{8,10},{10,12},{12,14},{1,3},{3,5},{5,7},{... | collective-permute-start | bytes 1198088 | tf_op jit(solution)/shard_map/ppermute | solution.py:23
  10.0 2.8 %collective-permute-done.1 = f32[64,2,1,4,128]{4,0,3,2,1:T(8,128)S(1)} collective-permute-done((f32[64,2,1,4,128]{4,0,3,2,1:T(8,128)S(1)}, f32[64,2,1,4,128]{4,0,3,2,1:T(8,128)S(1)}, u32[]{:S(2)}, u32[]{:S(2)}) %collective-permute-start.1) | collective-permute-done | bytes 262176 | tf_op jit(solution)/shard_map/ppermute | solution.py:26
  12.9 9.6 %collective-permute-done = f32[65,3,1,4,128]{4,0,3,2,1:T(8,128)S(1)} collective-permute-done((f32[65,3,1,4,128]{4,0,3,2,1:T(8,128)S(1)}, f32[65,3,1,4,128]{4,0,3,2,1:T(8,128)S(1)}, u32[]{:S(2)}, u32[]{:S(2)}) %collective-permute-start) | collective-permute-done | bytes 399392 | tf_op jit(solution)/shard_map/ppermute | solution.py:23
  22.6 1.3 %collective-permute-start.3 = (f32[64,2,3,1,128]{4,0,3,2,1:T(8,128)S(1)}, f32[64,2,3,1,128]{4,0,3,2,1:T(8,128)S(1)}, u32[]{:S(2)}, u32[]{:S(2)}) collective-permute-start(f32[64,2,3,1,128]{4,0,3,2,1:T(8,128)S(1)} %fusion.16), channel_id=1, source_target_pairs={{1,0},{3,2},{5,4},{7,6},{9,8},{11,10},{13,12},{15,14},{17,16},{19,... | collective-permute-start | bytes 589832 | tf_op jit(solution)/shard_map/ppermute | solution.py:26
  23.9 3.1 %collective-permute-start.2 = (f32[65,3,3,1,128]{4,0,3,2,1:T(8,128)S(1)}, f32[65,3,3,1,128]{4,0,3,2,1:T(8,128)S(1)}, u32[]{:S(2)}, u32[]{:S(2)}) collective-permute-start(f32[65,3,3,1,128]{4,0,3,2,1:T(8,128)S(1)} %fusion.9), channel_id=1, source_target_pairs={{0,1},{2,3},{4,5},{6,7},{8,9},{10,11},{12,13},{14,15},{16,17},{18,... | collective-permute-start | bytes 898568 | tf_op jit(solution)/shard_map/ppermute | solution.py:23
  27.6 0.6 collective-permute-done.2
  30.0 2.9 %collective-permute-start.4 = (f32[2,64,64]{1,2,0:T(8,128)S(1)}, f32[2,64,64]{1,2,0:T(8,128)S(1)}, u32[]{:S(2)}, u32[]{:S(2)}) collective-permute-start(f32[2,64,64]{1,2,0:T(8,128)S(1)} %pad_maximum_fusion.3), channel_id=1, source_target_pairs={{0,8},{1,9},{2,10},{3,11},{4,12},{5,13},{6,14},{7,15},{8,0},{9,1},... | collective-permute-start | bytes 98312 | tf_op jit(solution)/shard_map/ppermute | solution.py:97
  33.0 4.0 %collective-permute-done.4 = f32[2,64,64]{1,2,0:T(8,128)S(1)} collective-permute-done((f32[2,64,64]{1,2,0:T(8,128)S(1)}, f32[2,64,64]{1,2,0:T(8,128)S(1)}, u32[]{:S(2)}, u32[]{:S(2)}) %collective-permute-start.4) | collective-permute-done | bytes 32800 | tf_op jit(solution)/shard_map/ppermute | solution.py:97
  37.0 0.8 %collective-permute-start.5 = (f32[2,64,64]{1,2,0:T(8,128)S(1)}, f32[2,64,64]{1,2,0:T(8,128)S(1)}, u32[]{:S(2)}, u32[]{:S(2)}) collective-permute-start(f32[2,64,64]{1,2,0:T(8,128)S(1)} %fusion.30), channel_id=1, source_target_pairs={{0,4},{1,5},{2,6},{3,7},{4,0},{5,1},{6,2},{7,3},{8,12},{9,13},{10,... | collective-permute-start | bytes 98312 | tf_op jit(solution)/shard_map/ppermute | solution.py:97
  37.8 3.5 %collective-permute-done.5 = f32[2,64,64]{1,2,0:T(8,128)S(1)} collective-permute-done((f32[2,64,64]{1,2,0:T(8,128)S(1)}, f32[2,64,64]{1,2,0:T(8,128)S(1)}, u32[]{:S(2)}, u32[]{:S(2)}) %collective-permute-start.5) | collective-permute-done | bytes 32800 | tf_op jit(solution)/shard_map/ppermute | solution.py:97
  41.4 2.3 %collective-permute-start.6 = (f32[2,64,64]{1,2,0:T(8,128)S(1)}, f32[2,64,64]{1,2,0:T(8,128)S(1)}, u32[]{:S(2)}, u32[]{:S(2)}) collective-permute-start(f32[2,64,64]{1,2,0:T(8,128)S(1)} %fusion.36), channel_id=1, source_target_pairs={{0,2},{1,3},{2,0},{3,1},{4,6},{5,7},{6,4},{7,5},{8,10},{9,11},{10,... | collective-permute-start | bytes 98312 | tf_op jit(solution)/shard_map/ppermute | solution.py:97
  43.7 2.2 %collective-permute-done.6 = f32[2,64,64]{1,2,0:T(8,128)S(1)} collective-permute-done((f32[2,64,64]{1,2,0:T(8,128)S(1)}, f32[2,64,64]{1,2,0:T(8,128)S(1)}, u32[]{:S(2)}, u32[]{:S(2)}) %collective-permute-start.6) | collective-permute-done | bytes 32800 | tf_op jit(solution)/shard_map/ppermute | solution.py:97
  47.4 5.8 %cholesky.17 = f32[64,64]{1,0:T(8,128)S(1)} custom-call(f32[64,64]{1,0:T(8,128)S(1)} %fusion.24), custom_call_target="Cholesky" | custom-call | tf_op jit(solution)/shard_map/jit(cholesky)/cholesky | solution.py:119
  53.3 0.6 compare_reduce_fusion
  53.9 0.7 %fusion.29 = (f32[64,64]{0,1:T(8,128)S(1)}, f32[1,64,64]{2,1,0:T(8,128)S(1)}) fusion(f32[64,64]{1,0:T(8,128)S(1)} %cholesky.17, pred[]{:T(512)} %compare_reduce_fusion), kind=kLoop, calls=%fused_computation.64 | loop fusion | flops 16384 | bytes 49153 | tf_op jit(solution)/shard_map/transpose | solution.py:123
  54.6 0.7 %copy.111 = f32[64,64]{1,0:T(8,128)} copy(f32[64,64]{0,1:T(8,128)S(1)} %get-tuple-element.37) | data formatting | bytes 32768
  55.3 4.9 %custom-call.6 = f32[1,64,64]{1,2,0:T(8,128)S(1)} custom-call(f32[1,64,64]{2,1,0:T(8,128)S(1)} %get-tuple-element.38), custom_call_target="InvertDiagBlocksLowerTriangular" | custom-call | tf_op jit(solution)/shard_map/triangular_solve | solution.py:120
  60.6 0.8 %fusion.32 = f32[64,64]{1,0:T(8,128)} fusion(f32[64,64]{1,0:T(8,128)S(1)} %fusion.23, f32[64,64]{1,0:T(8,128)S(1)} %fusion.27), kind=kOutput, calls=%fused_computation.76 | convolution fusion | flops 3145728 | bytes 49152 | tf_op jit(solution)/shard_map/dot_general | solution.py:102
  61.9 0.5 convolution_bitcast_fusion.1
  62.3 1.0 %copy.110 = f32[64,3,1,4,128]{4,3,2,1,0:T(4,128)} copy(f32[64,3,1,4,128]{4,0,3,1,2:T(8,128)S(1)} %convolution_bitcast_fusion.1) | data formatting | bytes 786432
  63.3 1.0 %copy.112 = f32[64,3,1,4,128]{4,3,2,1,0:T(4,128)} copy(f32[64,3,1,4,128]{4,0,3,1,2:T(8,128)S(1)} %convolution_bitcast_fusion) | data formatting | bytes 786432
  (50 shorter events, 4.9 us)
Async XLA Ops:
  1.7 11.2 %collective-permute-start.1 = (f32[64,2,1,4,128]{4,0,3,2,1:T(8,128)S(1)}, f32[64,2,1,4,128]{4,0,3,2,1:T(8,128)S(1)}, u32[]{:S(2)}, u32[]{:S(2)}) collective-permute-start(f32[64,2,1,4,128]{4,0,3,2,1:T(8,128)S(1)} %concatenate.45), channel_id=1, source_target_pairs={{2,0},{4,2},{6,4},{8,6},{10,8},{12,10},{14,12},{3,1},{5,3},{7,5},{... | collective-permute-start | bytes 786440 | tf_op jit(solution)/shard_map/ppermute | solution.py:26
  3.8 18.7 %collective-permute-start = (f32[65,3,1,4,128]{4,0,3,2,1:T(8,128)S(1)}, f32[65,3,1,4,128]{4,0,3,2,1:T(8,128)S(1)}, u32[]{:S(2)}, u32[]{:S(2)}) collective-permute-start(f32[65,3,1,4,128]{4,0,3,2,1:T(8,128)S(1)} %pad_maximum_fusion), channel_id=1, source_target_pairs={{0,2},{2,4},{4,6},{6,8},{8,10},{10,12},{12,14},{1,3},{3,5},{5,7},{... | collective-permute-start | bytes 1198088 | tf_op jit(solution)/shard_map/ppermute | solution.py:23
  12.9 14.1 %copy-start = (f32[64,3,1,4,128]{4,3,2,1,0:T(4,128)S(1)}, f32[64,3,1,4,128]{4,3,2,1,0:T(4,128)}, u32[]{:S(2)}) copy-start(f32[64,3,1,4,128]{4,3,2,1,0:T(4,128)} %param.5) | copy-start | bytes 1179652
  22.6 5.0 %collective-permute-start.3 = (f32[64,2,3,1,128]{4,0,3,2,1:T(8,128)S(1)}, f32[64,2,3,1,128]{4,0,3,2,1:T(8,128)S(1)}, u32[]{:S(2)}, u32[]{:S(2)}) collective-permute-start(f32[64,2,3,1,128]{4,0,3,2,1:T(8,128)S(1)} %fusion.16), channel_id=1, source_target_pairs={{1,0},{3,2},{5,4},{7,6},{9,8},{11,10},{13,12},{15,14},{17,16},{19,... | collective-permute-start | bytes 589832 | tf_op jit(solution)/shard_map/ppermute | solution.py:26
  23.9 4.3 %collective-permute-start.2 = (f32[65,3,3,1,128]{4,0,3,2,1:T(8,128)S(1)}, f32[65,3,3,1,128]{4,0,3,2,1:T(8,128)S(1)}, u32[]{:S(2)}, u32[]{:S(2)}) collective-permute-start(f32[65,3,3,1,128]{4,0,3,2,1:T(8,128)S(1)} %fusion.9), channel_id=1, source_target_pairs={{0,1},{2,3},{4,5},{6,7},{8,9},{10,11},{12,13},{14,15},{16,17},{18,... | collective-permute-start | bytes 898568 | tf_op jit(solution)/shard_map/ppermute | solution.py:23
  30.0 7.0 %collective-permute-start.4 = (f32[2,64,64]{1,2,0:T(8,128)S(1)}, f32[2,64,64]{1,2,0:T(8,128)S(1)}, u32[]{:S(2)}, u32[]{:S(2)}) collective-permute-start(f32[2,64,64]{1,2,0:T(8,128)S(1)} %pad_maximum_fusion.3), channel_id=1, source_target_pairs={{0,8},{1,9},{2,10},{3,11},{4,12},{5,13},{6,14},{7,15},{8,0},{9,1},... | collective-permute-start | bytes 98312 | tf_op jit(solution)/shard_map/ppermute | solution.py:97
  37.0 4.3 %collective-permute-start.5 = (f32[2,64,64]{1,2,0:T(8,128)S(1)}, f32[2,64,64]{1,2,0:T(8,128)S(1)}, u32[]{:S(2)}, u32[]{:S(2)}) collective-permute-start(f32[2,64,64]{1,2,0:T(8,128)S(1)} %fusion.30), channel_id=1, source_target_pairs={{0,4},{1,5},{2,6},{3,7},{4,0},{5,1},{6,2},{7,3},{8,12},{9,13},{10,... | collective-permute-start | bytes 98312 | tf_op jit(solution)/shard_map/ppermute | solution.py:97
  41.4 4.6 %collective-permute-start.6 = (f32[2,64,64]{1,2,0:T(8,128)S(1)}, f32[2,64,64]{1,2,0:T(8,128)S(1)}, u32[]{:S(2)}, u32[]{:S(2)}) collective-permute-start(f32[2,64,64]{1,2,0:T(8,128)S(1)} %fusion.36), channel_id=1, source_target_pairs={{0,2},{1,3},{2,0},{3,1},{4,6},{5,7},{6,4},{7,5},{8,10},{9,11},{10,... | collective-permute-start | bytes 98312 | tf_op jit(solution)/shard_map/ppermute | solution.py:97
  45.9 1.3 %collective-permute-start.7 = (f32[2,64,64]{1,2,0:T(8,128)S(1)}, f32[2,64,64]{1,2,0:T(8,128)S(1)}, u32[]{:S(2)}, u32[]{:S(2)}) collective-permute-start(f32[2,64,64]{1,2,0:T(8,128)S(1)} %add.37), channel_id=1, source_target_pairs={{0,1},{1,0},{2,3},{3,2},{4,5},{5,4},{6,7},{7,6},{8,9},{9,8},{10,11... | collective-permute-start | bytes 98312 | tf_op jit(solution)/shard_map/ppermute | solution.py:97
